TPU v7x, 128 devices: a whole 4x4x4 slice. The times are simulated.
128 devices in a mesh: tok: 32 (over y, z, core), head: 4 (over x).
Axes of the slice: x: 4, y: 4, z: 4, core: 2. Of those that a mesh axis runs over, the one named last changes fastest.
Arguments:
- queries: bfloat16 [32768, 4096], P(('tok', 'head')), may hold values from -64 to 64
- keys: bfloat16 [32768, 4096], P(('tok', 'head')), may hold values from -6 to 6
- values: bfloat16 [32768, 4096], P(('tok', 'head')), may hold values from -6 to 6
- token_rates: bfloat16 [32768, 8], P(('tok', 'head')), may hold values from 0.099609375 to 1
- gate_start: bfloat16 [8, 512, 1024], P('head'), may hold values from -0.25 to 0.25
- up_start: bfloat16 [8, 512, 1024], P('head'), may hold values from -0.25 to 0.25
- down_start: bfloat16 [8, 1024, 512], P('head'), may hold values from -0.1875 to 0.1875
- norm_gain: float32 [4096], replicated, may hold values from 0.25 to 1.75
- bounds: int32 [16], replicated, may hold values from 896 to 1152
Outputs:
- layer_out: bfloat16 [32768, 4096], P(('tok', 'head'))
Inputs may be any that keep to these rules, and one draw needn't show every extreme that they name: The first span of segment s is its positions below bounds[s].
All inputs are finite; a program needn't handle non-finite values.
Results may differ from a plain program's by a relative error of at most 0.02.
Values may be sent and summed in bfloat16 or wider, within the bound.
No kernel may reach another device: no remote copies, remote signals or barrier semaphores. Data moves between devices by JAX's collectives and lax.ppermute only.
A program may use at most 192 MiB of HBM per device.

v0:
```python
import functools
import math

import jax
import jax.numpy as jnp
from jax import lax
from jax.experimental import pallas as pl
from jax.experimental.pallas import tpu as pltpu
from jax.sharding import PartitionSpec as P

FDIM = 512
HID = 1024
AHD = 128
WINDOW = 512
NS_ITERS = 3
LEN = 2048
HALF = 128
LOW = 896
HIGH = 1152
SPLIT = 8
BLOCK = LEN // SPLIT

linear_coef = 3.4445
cubic_coef = -4.775
quintic_coef = 2.0315
rms_epsilon = 1e-05
norm_epsilon = 1e-06
MASKED = -1e30
EXP2_SCALE = math.log2(math.e) / math.sqrt(AHD)

AXES = ("tok", "head")
F32 = jnp.float32
BF16 = jnp.bfloat16


def place_of(block):
    return (block % 4) * 2 + block // 4


def dot(a, b):
    return lax.dot_general(a, b, (((1,), (0,)), ((), ())), preferred_element_type=F32)


def dot_nt(a, b):
    return lax.dot_general(a, b, (((1,), (1,)), ((), ())), preferred_element_type=F32)


def update_kernel(
    scalars,
    k_hbm,
    v_hbm,
    rates,
    gate_hbm,
    up_hbm,
    down_hbm,
    new_gate,
    new_up,
    new_down,
    kbuf,
    vbuf,
    wg,
    wu,
    wd,
    wdt,
    hid,
    dgate,
    dup,
    target,
    kt,
    tt,
    grads,
    xs,
    grams,
    sems,
):
    bound = scalars[0]
    parity = scalars[1]
    owned = scalars[3]
    copies = []

    def fetch(src, dst):
        copy = pltpu.make_async_copy(src, dst, sems.at[len(copies)])
        copy.start()
        copies.append(copy)

    fetch(gate_hbm.at[parity], wg)
    fetch(up_hbm.at[parity], wu)
    fetch(down_hbm.at[parity], wd)
    for block in range(5):
        rows = min(BLOCK, HIGH - block * BLOCK)
        src = pl.ds(place_of(block) * BLOCK, rows)
        dst = pl.ds(block * BLOCK, rows)
        fetch(k_hbm.at[src], kbuf.at[dst])
        fetch(v_hbm.at[src], vbuf.at[dst])
    for copy in copies:
        copy.wait()

    wdt[...] = wd[...].T
    lane = lax.broadcasted_iota(jnp.int32, (1, 8), 1)
    pick = (lane == owned).astype(F32)
    step = 384
    for part in range(HIGH // step):
        rows = pl.ds(part * step, step)
        rate = jnp.sum(rates[rows, :].astype(F32) * pick, axis=1, keepdims=True)
        place = part * step + lax.broadcasted_iota(jnp.int32, (step, 1), 0)
        weighted = rate * vbuf[rows, :].astype(F32)
        target[rows, :] = jnp.where(place < bound, weighted, 0.0).astype(BF16)
        k_rows = kbuf[rows, :]
        t_rows = target[rows, :]
        for tile in range(HID // 256):
            cols = pl.ds(tile * 256, 256)
            pre_gate = dot(k_rows, wg[:, cols])
            pre_up = dot(k_rows, wu[:, cols])
            back = dot(t_rows, wdt[:, cols])
            logistic = 1.0 / (1.0 + jnp.exp(-pre_gate))
            act = pre_gate * logistic
            slope = logistic * (1.0 + pre_gate * (1.0 - logistic))
            hid[rows, cols] = (act * pre_up).astype(BF16)
            dgate[rows, cols] = (back * pre_up * slope).astype(BF16)
            dup[rows, cols] = (back * act).astype(BF16)
    kt[...] = kbuf[...].T
    tt[...] = target[...].T

    for which, (left, right) in enumerate(((kt, dgate), (kt, dup), (tt, hid))):
        total = jnp.zeros((1, 256), F32)
        for tile in range(HID // 256):
            cols = pl.ds(tile * 256, 256)
            grad = dot(left[...], right[:, cols])
            grads[which, :, cols] = grad
            total += jnp.sum(grad * grad, axis=0, keepdims=True)
        inv = 1.0 / jnp.sqrt(jnp.sum(total, axis=1, keepdims=True) + norm_epsilon)
        for tile in range(HID // 256):
            cols = pl.ds(tile * 256, 256)
            xs[which, :, cols] = (grads[which, :, cols] * inv).astype(BF16)

    def iteration(_, carry):
        for which in range(3):
            for tile in range(2):
                rows = pl.ds(tile * 256, 256)
                grams[which, :, rows] = dot_nt(xs[which], xs[which, rows, :]).astype(BF16)
        for which in range(3):
            gram = grams[which]
            for tile in range(2):
                cols = pl.ds(tile * 256, 256)
                mixed = cubic_coef * grams[which, :, cols].astype(F32) + quintic_coef * dot(
                    gram, grams[which, :, cols]
                )
                grams[3 + which, :, cols] = mixed.astype(BF16)
        for which in range(3):
            mix = grams[3 + which]
            for tile in range(4):
                cols = pl.ds(tile * 256, 256)
                old = xs[which, :, cols]
                xs[which, :, cols] = (linear_coef * old.astype(F32) + dot(mix, old)).astype(BF16)
        return carry

    lax.fori_loop(0, NS_ITERS, iteration, 0)

    for which, (start, out) in enumerate(((wg, new_gate), (wu, new_up))):
        for tile in range(HID // 256):
            cols = pl.ds(tile * 256, 256)
            wide = start[:, cols].astype(F32)
            moved = wide + xs[which, :, cols].astype(F32)
            aim = jnp.sqrt(jnp.sum(wide * wide, axis=0, keepdims=True) + norm_epsilon)
            actual = jnp.sqrt(jnp.sum(moved * moved, axis=0, keepdims=True) + norm_epsilon)
            out[:, cols] = (moved * (aim / actual)).astype(BF16)
    for tile in range(FDIM // 128):
        rows = pl.ds(tile * 128, 128)
        wide = wdt[rows, :].astype(F32)
        moved = wide + xs[2, rows, :].astype(F32)
        aim = jnp.sqrt(jnp.sum(wide * wide, axis=1, keepdims=True) + norm_epsilon)
        actual = jnp.sqrt(jnp.sum(moved * moved, axis=1, keepdims=True) + norm_epsilon)
        new_down[:, rows] = (moved * (aim / actual)).astype(BF16).T


def fast_update(scalars, k_item, v_item, rates, gate_start, up_start, down_start):
    hbm = pl.BlockSpec(memory_space=pltpu.HBM)
    vmem = pl.BlockSpec(memory_space=pltpu.VMEM)
    return pl.pallas_call(
        update_kernel,
        name="fast_update",
        out_shape=(
            jax.ShapeDtypeStruct((FDIM, HID), BF16),
            jax.ShapeDtypeStruct((FDIM, HID), BF16),
            jax.ShapeDtypeStruct((HID, FDIM), BF16),
        ),
        in_specs=[pl.BlockSpec(memory_space=pltpu.SMEM), hbm, hbm, vmem, hbm, hbm, hbm],
        out_specs=(vmem, vmem, vmem),
        scratch_shapes=[
            pltpu.VMEM((HIGH, FDIM), BF16),
            pltpu.VMEM((HIGH, FDIM), BF16),
            pltpu.VMEM((FDIM, HID), BF16),
            pltpu.VMEM((FDIM, HID), BF16),
            pltpu.VMEM((HID, FDIM), BF16),
            pltpu.VMEM((FDIM, HID), BF16),
            pltpu.VMEM((HIGH, HID), BF16),
            pltpu.VMEM((HIGH, HID), BF16),
            pltpu.VMEM((HIGH, HID), BF16),
            pltpu.VMEM((HIGH, FDIM), BF16),
            pltpu.VMEM((FDIM, HIGH), BF16),
            pltpu.VMEM((FDIM, HIGH), BF16),
            pltpu.VMEM((3, FDIM, HID), F32),
            pltpu.VMEM((3, FDIM, HID), BF16),
            pltpu.VMEM((6, FDIM, FDIM), BF16),
            pltpu.SemaphoreType.DMA((13,)),
        ],
        compiler_params=pltpu.CompilerParams(vmem_limit_bytes=48 * 1024 * 1024),
        cost_estimate=pl.CostEstimate(
            flops=20_000_000_000, bytes_accessed=12_000_000, transcendentals=1_200_000
        ),
    )(scalars, k_item, v_item, rates, gate_start, up_start, down_start)


def apply_kernel(
    chunk,
    scalars,
    q_hbm,
    k_hbm,
    v_hbm,
    hk_hbm,
    hv_hbm,
    gate_hbm,
    up_hbm,
    down_hbm,
    new_gate,
    new_up,
    new_down,
    gain,
    out,
    qc,
    kbuf,
    vbuf,
    wg,
    wu,
    wd,
    hid,
    raw,
    before,
    fast,
    sems,
):
    bound = scalars[0]
    parity = scalars[1]
    sequence = scalars[2]
    owned = scalars[3]
    copies = []

    def fetch(src, dst):
        copy = pltpu.make_async_copy(src, dst, sems.at[len(copies)])
        copy.start()
        copies.append(copy)

    for block in range(SPLIT):
        src = pl.ds(place_of(block) * BLOCK + chunk * HALF, HALF)
        fetch(q_hbm.at[src], qc.at[pl.ds(block * HALF, HALF)])
    fetch(gate_hbm.at[parity], wg)
    fetch(up_hbm.at[parity], wu)
    fetch(down_hbm.at[parity], wd)
    first = len(copies)
    fetch(hk_hbm, kbuf.at[pl.ds(0, WINDOW)])
    fetch(hv_hbm, vbuf.at[pl.ds(0, WINDOW)])
    for block in range(SPLIT):
        src = pl.ds(place_of(block) * BLOCK, BLOCK)
        dst = pl.ds(WINDOW + block * BLOCK, BLOCK)
        fetch(k_hbm.at[src], kbuf.at[dst])
        fetch(v_hbm.at[src], vbuf.at[dst])
    for copy in copies[:first]:
        copy.wait()

    def swiglu(rows, gate, up, down, store):
        in_rows = qc[rows, :]
        for tile in range(HID // 256):
            cols = pl.ds(tile * 256, 256)
            pre_gate = dot(in_rows, gate[:, cols])
            pre_up = dot(in_rows, up[:, cols])
            hid[pl.ds(0, rows.size), cols] = (
                pre_gate / (1.0 + jnp.exp(-pre_gate)) * pre_up
            ).astype(BF16)
        store(dot(hid[pl.ds(0, rows.size), :], down[...]))

    edge = 4 if chunk == 0 else 3
    old_rows = pl.ds(0, (edge + 1) * HALF)
    new_rows = pl.ds(edge * HALF, (SPLIT - edge) * HALF)

    def store_old(value):
        raw[pl.ds(0, edge * HALF), :] = value[: edge * HALF]
        before[...] = value[edge * HALF :]

    def store_new(value):
        raw[new_rows, :] = value

    swiglu(old_rows, wg, wu, wd, store_old)
    swiglu(new_rows, new_gate, new_up, new_down, store_new)
    mid = pl.ds(edge * HALF, HALF)
    place = edge * BLOCK + chunk * HALF + lax.broadcasted_iota(jnp.int32, (HALF, 1), 0)
    raw[mid, :] = jnp.where(place < bound, before[...], raw[mid, :])
    gain_row = gain[pl.ds(owned, 1), :]
    for block in range(SPLIT):
        rows = pl.ds(block * HALF, HALF)
        value = raw[rows, :]
        root = jnp.sqrt(jnp.mean(value * value, axis=1, keepdims=True) + rms_epsilon)
        fast[rows, :] = (value / root * gain_row).astype(BF16)
    for copy in copies[first:]:
        copy.wait()

    row_iota = lax.broadcasted_iota(jnp.int32, (HALF, HALF), 0)
    col_iota = lax.broadcasted_iota(jnp.int32, (HALF, HALF), 1)
    keep_old = col_iota > row_iota
    keep_own = col_iota <= row_iota

    def attend(block, edge_block):
        base = pl.multiple_of(block * BLOCK + chunk * HALF, HALF)
        q_rows = pl.ds(pl.multiple_of(block * HALF, HALF), HALF)
        o_rows = pl.ds(pl.multiple_of(place_of(block) * HALF, HALF), HALF)
        keys = pl.ds(base, WINDOW + HALF)
        for head in range(FDIM // AHD):
            cols = pl.ds(head * AHD, AHD)
            scores = dot_nt(qc[q_rows, cols], kbuf[keys, cols])
            parts = [scores[:, i * HALF : (i + 1) * HALF] for i in range(5)]
            parts[0] = jnp.where(keep_old, parts[0], MASKED)
            parts[4] = jnp.where(keep_own, parts[4], MASKED)
            if edge_block:
                for i in range(4):
                    absent = (sequence == 0) & (base + i * HALF < WINDOW)
                    parts[i] = jnp.where(absent, MASKED, parts[i])
            masked = jnp.concatenate(parts, axis=1)
            top = jnp.max(masked, axis=1, keepdims=True)
            weights = jnp.exp2((masked - top) * EXP2_SCALE)
            total = jnp.sum(weights, axis=1, keepdims=True)
            mixed = dot(weights.astype(BF16), vbuf[keys, cols])
            attn = (mixed / total).astype(BF16)
            out[o_rows, cols] = (attn.astype(F32) + fast[q_rows, cols].astype(F32)).astype(BF16)

    def edge_body(block, carry):
        attend(block, True)
        return carry

    def main_body(block, carry):
        attend(block, False)
        return carry

    lax.fori_loop(0, 2, edge_body, 0)
    lax.fori_loop(2, SPLIT, main_body, 0)


def apply_chunk(
    chunk, scalars, q_item, k_item, v_item, halo_k, halo_v, starts, news, gain
):
    hbm = pl.BlockSpec(memory_space=pltpu.HBM)
    vmem = pl.BlockSpec(memory_space=pltpu.VMEM)
    rows = SPLIT * HALF
    return pl.pallas_call(
        functools.partial(apply_kernel, chunk),
        name="apply_attend",
        out_shape=jax.ShapeDtypeStruct((rows, FDIM), BF16),
        in_specs=[pl.BlockSpec(memory_space=pltpu.SMEM)] + [hbm] * 8 + [vmem] * 4,
        out_specs=vmem,
        scratch_shapes=[
            pltpu.VMEM((rows, FDIM), BF16),
            pltpu.VMEM((WINDOW + LEN, FDIM), BF16),
            pltpu.VMEM((WINDOW + LEN, FDIM), BF16),
            pltpu.VMEM((FDIM, HID), BF16),
            pltpu.VMEM((FDIM, HID), BF16),
            pltpu.VMEM((HID, FDIM), BF16),
            pltpu.VMEM((5 * HALF, HID), BF16),
            pltpu.VMEM((rows, FDIM), F32),
            pltpu.VMEM((HALF, FDIM), F32),
            pltpu.VMEM((rows, FDIM), BF16),
            pltpu.SemaphoreType.DMA((29,)),
        ],
        compiler_params=pltpu.CompilerParams(vmem_limit_bytes=40 * 1024 * 1024),
        cost_estimate=pl.CostEstimate(
            flops=8_000_000_000, bytes_accessed=14_000_000, transcendentals=4_000_000
        ),
    )(scalars, q_item, k_item, v_item, halo_k, halo_v, *starts, *news, gain)


def body(queries, keys, values, token_rates, gate_start, up_start, down_start, norm_gain, bounds):
    shards = lax.axis_size("tok") * lax.axis_size("head")
    column = lax.axis_index("head")
    parity = lax.axis_index("tok") % 2
    owned = 2 * column + parity
    sequence = lax.axis_index("tok") // 2
    groups = [
        [s * SPLIT + (i % 2) * 4 + i // 2 for i in range(SPLIT)] for s in range(shards // SPLIT)
    ]
    plain_groups = [[s * SPLIT + i for i in range(SPLIT)] for s in range(shards // SPLIT)]
    span_bound = lax.dynamic_index_in_dim(bounds, sequence, 0, keepdims=False)
    scalars = jnp.stack([span_bound, parity, sequence, owned]).astype(jnp.int32)

    def spread(array):
        return lax.all_to_all(
            array, AXES, split_axis=1, concat_axis=0, tiled=True, axis_index_groups=groups
        )

    def halo(item):
        tail = jnp.concatenate(
            [item[place_of(b) * BLOCK : (place_of(b) + 1) * BLOCK] for b in (6, 7)], axis=0
        )
        count = lax.axis_size("tok")
        return lax.ppermute(tail, "tok", [(i, i + 2) for i in range(count - 2)])

    rates = lax.all_gather(token_rates, AXES, axis=0, tiled=True, axis_index_groups=plain_groups)
    keys, rates = lax.optimization_barrier((keys, rates))
    k_item = spread(keys)
    v_item = spread(values)
    halo_k = halo(k_item)
    halo_v = halo(v_item)
    q_item = spread(queries)
    starts = (gate_start, up_start, down_start)
    news = fast_update(scalars, k_item, v_item, rates, *starts)
    gain = norm_gain.reshape(-1, FDIM)
    returned = []
    for chunk in range(2):
        out = apply_chunk(
            chunk, scalars, q_item, k_item, v_item, halo_k, halo_v, starts, news, gain
        )
        returned.append(
            lax.all_to_all(
                out, AXES, split_axis=0, concat_axis=1, tiled=True, axis_index_groups=groups
            )
        )
    return jnp.concatenate(returned, axis=0)


def solution(mesh):
    tokens = P(AXES, None)
    return jax.shard_map(
        body,
        mesh=mesh,
        in_specs=(
            tokens,
            tokens,
            tokens,
            tokens,
            P("head", None, None),
            P("head", None, None),
            P("head", None, None),
            P(),
            P(),
        ),
        out_specs=tokens,
        check_vma=False,
    )
```

profile of v0, /device:TPU:1, one launch (start us, length us, event | category | flops | bytes accessed | tf_op | source)
XLA Modules:
  0.0 210.7 jit_solution(16311558459058389885)
XLA Ops:
  0.0 0.8 copy.15
  0.8 24.7 %all_gather.3.rates = bf16[2048,8]{1,0:T(8,128)(2,1)S(1)} all-gather(bf16[256,8]{1,0:T(8,128)(2,1)S(1)} %copy.15), channel_id=1, replica_groups={{0,1,2,3,4,5,6,7},{8,9,10,11,12,13,14,15},{16,17,18,19,20,21,22,23},{24..., dimensions={0}, use_global_device_ids=true | all-gather | bytes 36864 | tf_op jit(solution)/shard_map/all_gather | solution.py:403
  25.5 3.3 %copy.16 = bf16[256,4096]{0,1:T(8,128)(2,1)S(1)} copy(bf16[256,4096]{1,0:T(8,128)(2,1)} %param.10) | data formatting | bytes 4194304 | tf_op jit(solution)/shard_map/optimization_barrier | solution.py:404
  28.8 2.4 %copy.17 = bf16[256,8,512]{2,0,1:T(8,128)(2,1)} copy(bf16[256,8,512]{0,2,1:T(8,128)(2,1)S(1)} %bitcast.39) | data formatting | bytes 4194304 | tf_op jit(solution)/shard_map/all_to_all | solution.py:392
  31.2 4.1 %all-to-all-start.1 = ((bf16[256,8,512]{2,0,1:T(8,128)(2,1)}), bf16[256,8,512]{2,0,1:T(8,128)(2,1)S(1)}, u32[]{:S(2)}, u32[]{:S(2)}) async-start(bf16[256,8,512]{2,0,1:T(8,128)(2,1)} %copy.17), calls=%async_computation.1 | async-start | bytes 4194304 | tf_op jit(solution)/shard_map/all_to_all | solution.py:392
  35.3 4.1 %copy.18 = bf16[256,4096]{0,1:T(8,128)(2,1)} copy(bf16[256,4096]{1,0:T(8,128)(2,1)} %param.11) | data formatting | bytes 4194304 | tf_op args[2]
  39.4 3.9 %copy.19 = bf16[256,8,512]{2,0,1:T(8,128)(2,1)} copy(bf16[256,8,512]{0,2,1:T(8,128)(2,1)} %bitcast.40) | data formatting | bytes 4194304 | tf_op jit(solution)/shard_map/all_to_all | solution.py:392
  43.3 18.4 %all-to-all-done.1 = bf16[256,8,512]{2,0,1:T(8,128)(2,1)S(1)} async-done(((bf16[256,8,512]{2,0,1:T(8,128)(2,1)}), bf16[256,8,512]{2,0,1:T(8,128)(2,1)S(1)}, u32[]{:S(2)}, u32[]{:S(2)}) %all-to-all-start.1) | async-done | bytes 2097184 | tf_op jit(solution)/shard_map/all_to_all | solution.py:392
  61.7 5.1 %all-to-all-start.2 = ((bf16[256,8,512]{2,0,1:T(8,128)(2,1)}), bf16[256,8,512]{2,0,1:T(8,128)(2,1)}, u32[]{:S(2)}, u32[]{:S(2)}) async-start(bf16[256,8,512]{2,0,1:T(8,128)(2,1)} %copy.19), calls=%async_computation.2 | async-start | bytes 4194304 | tf_op jit(solution)/shard_map/all_to_all | solution.py:392
  66.8 0.0 copy-done.11
  66.8 0.0 copy-start.12
  66.8 3.1 %copy.26 = bf16[32,8,8,512]{3,2,0,1:T(8,128)(2,1)} copy(bf16[32,8,8,512]{3,2,1,0:T(8,128)(2,1)} %bitcast.44) | data formatting | bytes 4194304 | tf_op jit(solution)/shard_map/all_to_all | solution.py:392
  69.9 0.0 copy-done.12
  69.9 0.6 dynamic_slice.4
  70.5 0.6 pad_add_fusion.scalars
  71.2 0.8 pad_maximum_fusion.1
  72.0 3.6 %collective-permute-start = (bf16[512,512]{1,0:T(8,128)(2,1)}, bf16[512,512]{1,0:T(8,128)(2,1)S(1)}, u32[]{:S(2)}, u32[]{:S(2)}) collective-permute-start(bf16[512,512]{1,0:T(8,128)(2,1)} %pad_maximum_fusion.1), channel_id=1, source_target_pairs={{0,8},{4,12},{8,16},{12,20},{16,24},{20,28},{24,32},{28,36},{32,40... | collective-permute-start | bytes 1572872 | tf_op jit(solution)/shard_map/ppermute | solution.py:401
  75.6 17.7 %all-to-all-done.2 = bf16[256,8,512]{2,0,1:T(8,128)(2,1)} async-done(((bf16[256,8,512]{2,0,1:T(8,128)(2,1)}), bf16[256,8,512]{2,0,1:T(8,128)(2,1)}, u32[]{:S(2)}, u32[]{:S(2)}) %all-to-all-start.2) | async-done | bytes 2097184 | tf_op jit(solution)/shard_map/all_to_all | solution.py:392
  93.2 5.1 %all-to-all-start = ((bf16[256,8,512]{2,0,1:T(8,128)(2,1)}), bf16[256,8,512]{2,0,1:T(8,128)(2,1)}, u32[]{:S(2)}, u32[]{:S(2)}) async-start(bf16[256,8,512]{2,0,1:T(8,128)(2,1)} %bitcast.38), calls=%async_computation | async-start | bytes 4194304 | tf_op jit(solution)/shard_map/all_to_all | solution.py:392
  98.3 1.1 slice_bitcast_fusion.1
  99.4 0.8 pad_maximum_fusion.2
  100.2 4.4 %collective-permute-start.1 = (bf16[512,512]{1,0:T(8,128)(2,1)}, bf16[512,512]{1,0:T(8,128)(2,1)}, u32[]{:S(2)}, u32[]{:S(2)}) collective-permute-start(bf16[512,512]{1,0:T(8,128)(2,1)} %pad_maximum_fusion.2), channel_id=1, source_target_pairs={{0,8},{4,12},{8,16},{12,20},{16,24},{20,28},{24,32},{28,36},{32,40... | collective-permute-start | bytes 1572872 | tf_op jit(solution)/shard_map/ppermute | solution.py:401
  104.6 27.9 %fast_update.1 = (bf16[512,1024]{1,0:T(8,128)(2,1)S(1)}, bf16[512,1024]{1,0:T(8,128)(2,1)S(1)}, bf16[1024,512]{1,0:T(8,128)(2,1)S(1)}) custom-call(s32[4]{0:T(128)S(1)} %pad_add_fusion.scalars, bf16[2048,512]{1,0:T(8,128)(2,1)S(1)} %bitcast.35, bf16[2048,512]{1,0:T(8,128)(2,1)} %bitcast.10.v_hbm, bf16[2048,8]{1,0:T(8,128)(2,1)S(1)} %all_gather.3.rates, ...), custom_call_target="tpu_custom_call" | custom-call | flops 20000000000 | bytes 12000000 | tf_op jit(solution)/shard_map/fast_update/pallas_call | solution.py:179
  132.6 0.0 copy-start.2
  132.6 1.0 copy-done.2
  133.5 1.0 copy-done.5
  134.5 1.1 copy-done.8
  135.6 0.0 all-to-all-done
  135.6 0.0 collective-permute-done.hk_hbm
  135.6 0.0 collective-permute-done.1.hv_hbm
  135.6 0.0 copy-start
  135.6 1.6 copy-done
  137.2 1.2 copy-done.3
  138.4 1.2 copy-done.6
  139.6 1.2 copy-done.9
  140.9 18.9 %apply_attend.3 = bf16[1024,512]{1,0:T(8,128)(2,1)} custom-call(s32[4]{0:T(128)S(1)} %pad_add_fusion.scalars, bf16[2048,512]{1,0:T(8,128)(2,1)} %bitcast.4.q_hbm, bf16[2048,512]{1,0:T(8,128)(2,1)S(1)} %bitcast.36, bf16[2048,512]{1,0:T(8,128)(2,1)} %bitcast.10.v_hbm, bf16[512,512]{1,0:T(8,128)(2,1)S(1)} %collective-permute-done.hk_hbm, ...), custom_call_target="tpu_custom_call" | custom-call | flops 8000000000 | bytes 14000000 | tf_op jit(solution)/shard_map/apply_attend/pallas_call | solution.py:352
  159.8 5.1 %all-to-all-start.4 = ((bf16[8,128,512]{2,1,0:T(8,128)(2,1)}), bf16[8,128,512]{2,1,0:T(8,128)(2,1)}, u32[]{:S(2)}, u32[]{:S(2)}) async-start(bf16[8,128,512]{2,1,0:T(8,128)(2,1)} %bitcast.20), calls=%async_computation.4 | async-start | bytes 2097152 | tf_op jit(solution)/shard_map/all_to_all | solution.py:419
  164.9 1.6 copy-done.1
  166.5 1.2 copy-done.4
  167.7 1.2 copy-done.7
  168.9 1.2 copy-done.10
  170.2 19.0 %apply_attend.2 = bf16[1024,512]{1,0:T(8,128)(2,1)} custom-call(s32[4]{0:T(128)S(1)} %pad_add_fusion.scalars, bf16[2048,512]{1,0:T(8,128)(2,1)} %bitcast.4.q_hbm, bf16[2048,512]{1,0:T(8,128)(2,1)S(1)} %bitcast.37, bf16[2048,512]{1,0:T(8,128)(2,1)} %bitcast.10.v_hbm, bf16[512,512]{1,0:T(8,128)(2,1)S(1)} %collective-permute-done.hk_hbm, ...), custom_call_target="tpu_custom_call" | custom-call | flops 8000000000 | bytes 14000000 | tf_op jit(solution)/shard_map/apply_attend/pallas_call | solution.py:352
  189.1 0.0 all-to-all-done.4
  189.1 4.8 %all-to-all-start.3 = ((bf16[8,128,512]{2,1,0:T(8,128)(2,1)}), bf16[8,128,512]{2,1,0:T(8,128)(2,1)S(1)}, u32[]{:S(2)}, u32[]{:S(2)}) async-start(bf16[8,128,512]{2,1,0:T(8,128)(2,1)} %bitcast.17), calls=%async_computation.3 | async-start | bytes 2097152 | tf_op jit(solution)/shard_map/all_to_all | solution.py:419
  193.9 1.3 copy.24
  195.3 13.8 %all-to-all-done.3 = bf16[8,128,512]{2,1,0:T(8,128)(2,1)S(1)} async-done(((bf16[8,128,512]{2,1,0:T(8,128)(2,1)}), bf16[8,128,512]{2,1,0:T(8,128)(2,1)S(1)}, u32[]{:S(2)}, u32[]{:S(2)}) %all-to-all-start.3) | async-done | bytes 1048608 | tf_op jit(solution)/shard_map/all_to_all | solution.py:419
  209.0 0.1 copy.23
  209.1 1.5 pad_maximum_fusion
  (12 shorter events, 0.1 us)
Async XLA Ops:
  31.2 30.5 %all-to-all-start.1 = ((bf16[256,8,512]{2,0,1:T(8,128)(2,1)}), bf16[256,8,512]{2,0,1:T(8,128)(2,1)S(1)}, u32[]{:S(2)}, u32[]{:S(2)}) async-start(bf16[256,8,512]{2,0,1:T(8,128)(2,1)} %copy.17), calls=%async_computation.1 | async-start | bytes 4194304 | tf_op jit(solution)/shard_map/all_to_all | solution.py:392
  43.3 23.5 %copy-start.11 = (f32[4096]{0:T(1024)S(1)}, f32[4096]{0:T(1024)}, u32[]{:S(2)}) copy-start(f32[4096]{0:T(1024)} %param.16) | copy-start | bytes 49156
  61.7 31.5 %all-to-all-start.2 = ((bf16[256,8,512]{2,0,1:T(8,128)(2,1)}), bf16[256,8,512]{2,0,1:T(8,128)(2,1)}, u32[]{:S(2)}, u32[]{:S(2)}) async-start(bf16[256,8,512]{2,0,1:T(8,128)(2,1)} %copy.19), calls=%async_computation.2 | async-start | bytes 4194304 | tf_op jit(solution)/shard_map/all_to_all | solution.py:392
  66.8 3.1 %copy-start.12 = (s32[16]{0:T(128)S(1)}, s32[16]{0:T(128)}, u32[]{:S(2)}) copy-start(s32[16]{0:T(128)} %param.17) | copy-start | bytes 196
  72.0 63.6 %collective-permute-start = (bf16[512,512]{1,0:T(8,128)(2,1)}, bf16[512,512]{1,0:T(8,128)(2,1)S(1)}, u32[]{:S(2)}, u32[]{:S(2)}) collective-permute-start(bf16[512,512]{1,0:T(8,128)(2,1)} %pad_maximum_fusion.1), channel_id=1, source_target_pairs={{0,8},{4,12},{8,16},{12,20},{16,24},{20,28},{24,32},{28,36},{32,40... | collective-permute-start | bytes 1572872 | tf_op jit(solution)/shard_map/ppermute | solution.py:401
  93.2 42.3 %all-to-all-start = ((bf16[256,8,512]{2,0,1:T(8,128)(2,1)}), bf16[256,8,512]{2,0,1:T(8,128)(2,1)}, u32[]{:S(2)}, u32[]{:S(2)}) async-start(bf16[256,8,512]{2,0,1:T(8,128)(2,1)} %bitcast.38), calls=%async_computation | async-start | bytes 4194304 | tf_op jit(solution)/shard_map/all_to_all | solution.py:392
  100.2 35.4 %collective-permute-start.1 = (bf16[512,512]{1,0:T(8,128)(2,1)}, bf16[512,512]{1,0:T(8,128)(2,1)}, u32[]{:S(2)}, u32[]{:S(2)}) collective-permute-start(bf16[512,512]{1,0:T(8,128)(2,1)} %pad_maximum_fusion.2), channel_id=1, source_target_pairs={{0,8},{4,12},{8,16},{12,20},{16,24},{20,28},{24,32},{28,36},{32,40... | collective-permute-start | bytes 1572872 | tf_op jit(solution)/shard_map/ppermute | solution.py:401
  132.6 1.0 copy-start.2
  133.5 1.0 copy-start.5
  134.5 1.1 copy-start.8
  135.6 1.6 copy-start
  137.2 1.2 copy-start.3
  138.4 1.2 copy-start.6
  139.6 1.2 copy-start.9
  159.8 29.3 %all-to-all-start.4 = ((bf16[8,128,512]{2,1,0:T(8,128)(2,1)}), bf16[8,128,512]{2,1,0:T(8,128)(2,1)}, u32[]{:S(2)}, u32[]{:S(2)}) async-start(bf16[8,128,512]{2,1,0:T(8,128)(2,1)} %bitcast.20), calls=%async_computation.4 | async-start | bytes 2097152 | tf_op jit(solution)/shard_map/all_to_all | solution.py:419
  164.9 1.6 copy-start.1
  166.5 1.2 copy-start.4
  167.7 1.2 copy-start.7
  168.9 1.2 copy-start.10
  189.1 19.9 %all-to-all-start.3 = ((bf16[8,128,512]{2,1,0:T(8,128)(2,1)}), bf16[8,128,512]{2,1,0:T(8,128)(2,1)S(1)}, u32[]{:S(2)}, u32[]{:S(2)}) async-start(bf16[8,128,512]{2,1,0:T(8,128)(2,1)} %bitcast.17), calls=%async_computation.3 | async-start | bytes 2097152 | tf_op jit(solution)/shard_map/all_to_all | solution.py:419
where the time goes:
time: 212 us; the launch traced here: 211 us
  Pallas kernels  65.8 us (31%)
  waiting for transfers between devices  49.8 us (23%)
  local copies, waits for them, and re-layouts  34.2 us (16%)
  starting transfers between devices  32.2 us (15%)
  blocking collectives  24.7 us (12%)
  other arithmetic  3.84 us (2%)
    pallas_call x2, Pallas kernels, apply_chunk(): pl.pallas_call(functools.partial(apply_kernel, chunk), name='apply_attend...  37.9 us
    all_to_all x3, waiting for transfers between devices, spread(): lax.all_to_all(array, AXES, split_axis=1, concat_axis=0, tiled=True, axis...  36 us
    pallas_call x1, Pallas kernels, fast_update(): pl.pallas_call(update_kernel, name='fast_update', out_shape=(jax.ShapeDty...  27.9 us
    all_gather x1, blocking collectives, body(): lax.all_gather(token_rates, AXES, axis=0, tiled=True, axis_index_groups=p...  24.7 us
    unnamed x28, local copies, waits for them, and re-layouts  18.4 us
    all_to_all x3, starting transfers between devices, spread(): lax.all_to_all(array, AXES, split_axis=1, concat_axis=0, tiled=True, axis...  14.3 us
    all_to_all x2, waiting for transfers between devices, body(): lax.all_to_all(out, AXES, split_axis=0, concat_axis=1, tiled=True, axis_i...  13.8 us
    all_to_all x2, starting transfers between devices, body(): lax.all_to_all(out, AXES, split_axis=0, concat_axis=1, tiled=True, axis_i...  9.9 us
  transfers between devices with their start and end apart: 7, of which 3 were waited for; matrix products, arithmetic and copies ran while one was open for 8% of the time, Pallas kernels for 22%

commit v1 on v0

--- a/solution.py
+++ b/solution.py
@@ -33,8 +33,135 @@
 BF16 = jnp.bfloat16
 
 
+CHIPS = 4
+KV_ROWS = 528
+RATE_ROW = 512
+VMEM_LIMIT = 60 * 1024 * 1024
+
+
 def place_of(block):
-    return (block % 4) * 2 + block // 4
+    return (block % CHIPS) * 2 + block // CHIPS
+
+
+class Fetcher:
+    def __init__(self, sems):
+        self.sems = sems
+        self.copies = []
+
+    def __call__(self, src, dst):
+        copy = pltpu.make_async_copy(src, dst, self.sems.at[len(self.copies)])
+        copy.start()
+        self.copies.append(copy)
+
+    def choose(self, options, dst):
+        sem = self.sems.at[len(self.copies)]
+        for cond, src in options:
+
+            @pl.when(cond)
+            def _(src=src):
+                pltpu.make_async_copy(src, dst, sem).start()
+
+        self.copies.append(pltpu.make_async_copy(options[0][1], dst, sem))
+
+    def wait(self, first=0, last=None):
+        for copy in self.copies[first:last]:
+            copy.wait()
+
+
+def position():
+    column = lax.axis_index("head")
+    tok = lax.axis_index("tok")
+    return column, lax.rem(tok, 2), lax.div(tok, 2)
+
+
+def pack_kv_kernel(keys, values, rates, *rest):
+    outs = rest[: CHIPS + 1]
+    kbuf, vbuf, lines, in_sems, sems = rest[CHIPS + 1 :]
+
+    def out_at(index):
+        return outs[index] if index < CHIPS else outs[CHIPS].at[index - CHIPS]
+
+    column, parity, _ = position()
+    load = Fetcher(in_sems)
+    fetch = Fetcher(sems)
+    load(keys, kbuf)
+    load(values, vbuf)
+    turned = rates[...].astype(F32)
+    place = lax.broadcasted_iota(jnp.int32, turned.shape, 0)
+    targets = []
+    for which in range(2):
+        core = parity if which == 0 else 1 - parity
+        for slot in range(CHIPS):
+            head = 2 * lax.rem(column + slot, CHIPS) + core
+            targets.append((which * CHIPS + slot, head))
+    for index, head in targets:
+        line = jnp.sum(jnp.where(place == head, turned, 0.0), axis=0, keepdims=True)
+        lines[index, :, pl.ds(0, BLOCK)] = jnp.broadcast_to(line, (16, BLOCK)).astype(BF16)
+        lines[index, :, pl.ds(BLOCK, FDIM - BLOCK)] = jnp.zeros((16, FDIM - BLOCK), BF16)
+    for index, head in targets:
+        fetch(lines.at[index], out_at(index).at[pl.ds(RATE_ROW, 16)])
+    for part, buf in ((0, kbuf), (1, vbuf)):
+        load.wait(part, part + 1)
+        for index, head in targets:
+            cols = pl.ds(pl.multiple_of(head * FDIM, FDIM), FDIM)
+            fetch(buf.at[:, cols], out_at(index).at[pl.ds(part * BLOCK, BLOCK)])
+    fetch.wait()
+
+
+def pack_kv(keys, values, rates):
+    hbm = pl.BlockSpec(memory_space=pltpu.HBM)
+    shape = jax.ShapeDtypeStruct((KV_ROWS, FDIM), BF16)
+    outs = pl.pallas_call(
+        pack_kv_kernel,
+        name="pack_kv",
+        out_shape=(shape,) * CHIPS + (jax.ShapeDtypeStruct((CHIPS, KV_ROWS, FDIM), BF16),),
+        in_specs=[hbm, hbm, pl.BlockSpec(memory_space=pltpu.VMEM)],
+        out_specs=(hbm,) * (CHIPS + 1),
+        scratch_shapes=[
+            pltpu.VMEM((BLOCK, CHIPS * 2 * FDIM), BF16),
+            pltpu.VMEM((BLOCK, CHIPS * 2 * FDIM), BF16),
+            pltpu.VMEM((2 * CHIPS, 16, FDIM), BF16),
+            pltpu.SemaphoreType.DMA((2,)),
+            pltpu.SemaphoreType.DMA((24,)),
+        ],
+        compiler_params=pltpu.CompilerParams(vmem_limit_bytes=VMEM_LIMIT),
+        cost_estimate=pl.CostEstimate(flops=0, bytes_accessed=16_000_000, transcendentals=0),
+    )(keys, values, rates)
+    return outs[:CHIPS], outs[CHIPS]
+
+
+def pack_q_kernel(queries, own, swap, qbuf, in_sems, sems):
+    column, parity, _ = position()
+    load = Fetcher(in_sems)
+    fetch = Fetcher(sems)
+    load(queries, qbuf)
+    load.wait()
+    for which in range(2):
+        core = parity if which == 0 else 1 - parity
+        for slot in range(CHIPS):
+            head = 2 * lax.rem(column + slot, CHIPS) + core
+            cols = pl.ds(pl.multiple_of(head * FDIM, FDIM), FDIM)
+            fetch(qbuf.at[:, cols], (own, swap)[which].at[slot])
+    fetch.wait()
+
+
+def pack_q(queries):
+    hbm = pl.BlockSpec(memory_space=pltpu.HBM)
+    shape = jax.ShapeDtypeStruct((CHIPS, BLOCK, FDIM), BF16)
+    return pl.pallas_call(
+        pack_q_kernel,
+        name="pack_q",
+        out_shape=(shape, shape),
+        in_specs=[hbm],
+        out_specs=(hbm, hbm),
+        scratch_shapes=[
+            pltpu.VMEM((BLOCK, CHIPS * 2 * FDIM), BF16),
+            pltpu.SemaphoreType.DMA((1,)),
+            pltpu.SemaphoreType.DMA((8,)),
+        ],
+        compiler_params=pltpu.CompilerParams(vmem_limit_bytes=VMEM_LIMIT),
+        cost_estimate=pl.CostEstimate(flops=0, bytes_accessed=8_000_000, transcendentals=0),
+    )(queries)
 
 
 def dot(a, b):
@@ -46,18 +173,27 @@
 
 
 def update_kernel(
-    scalars,
-    k_hbm,
-    v_hbm,
-    rates,
+    bounds,
+    own0,
+    own1,
+    own2,
+    own3,
+    other0,
+    other1,
+    other2,
+    other3,
     gate_hbm,
     up_hbm,
     down_hbm,
+    gate_out,
+    up_out,
+    down_out,
     new_gate,
     new_up,
     new_down,
     kbuf,
     vbuf,
+    rbuf,
     wg,
     wu,
     wd,
@@ -72,39 +208,54 @@
     xs,
     grams,
     sems,
+    out_sems,
 ):
-    bound = scalars[0]
-    parity = scalars[1]
-    owned = scalars[3]
-    copies = []
-
-    def fetch(src, dst):
-        copy = pltpu.make_async_copy(src, dst, sems.at[len(copies)])
-        copy.start()
-        copies.append(copy)
+    column, parity, sequence = position()
+    bound = bounds[sequence]
+    fetch = Fetcher(sems)
+    owns = (own0, own1, own2, own3)
+    others = (other0, other1, other2, other3)
+    core0, core1 = parity == 0, parity == 1
+
+    def low_part(rows, make_dst):
+        for slot in range(CHIPS):
+            source = lax.rem(column + CHIPS - slot, CHIPS)
+            fetch.choose(
+                [(core0, owns[slot].at[rows]), (core1, others[slot].at[rows])], make_dst(source)
+            )
+
+    def top_part(rows, dst):
+        options = []
+        for slot in range(CHIPS):
+            options.append((core0 & (column == slot), others[slot].at[rows]))
+            options.append((core1 & (column == slot), owns[slot].at[rows]))
+        fetch.choose(options, dst)
+
+    def rows_at(buf):
+        return lambda block: buf.at[pl.ds(pl.multiple_of(block * BLOCK, BLOCK), BLOCK)]
 
     fetch(gate_hbm.at[parity], wg)
     fetch(up_hbm.at[parity], wu)
+    low_part(pl.ds(0, BLOCK), rows_at(kbuf))
+    top_part(pl.ds(0, HALF), kbuf.at[pl.ds(CHIPS * BLOCK, HALF)])
     fetch(down_hbm.at[parity], wd)
-    for block in range(5):
-        rows = min(BLOCK, HIGH - block * BLOCK)
-        src = pl.ds(place_of(block) * BLOCK, rows)
-        dst = pl.ds(block * BLOCK, rows)
-        fetch(k_hbm.at[src], kbuf.at[dst])
-        fetch(v_hbm.at[src], vbuf.at[dst])
-    for copy in copies:
-        copy.wait()
+    low_part(pl.ds(BLOCK, BLOCK), rows_at(vbuf))
+    top_part(pl.ds(BLOCK, HALF), vbuf.at[pl.ds(CHIPS * BLOCK, HALF)])
+    low_part(pl.ds(RATE_ROW, 16), lambda block: rbuf.at[block])
+    top_part(pl.ds(RATE_ROW, 16), rbuf.at[CHIPS])
+    fetch.wait()
 
     wdt[...] = wd[...].T
-    lane = lax.broadcasted_iota(jnp.int32, (1, 8), 1)
-    pick = (lane == owned).astype(F32)
+    for block in range(CHIPS + 1):
+        count = min(BLOCK, HIGH - block * BLOCK)
+        rows = pl.ds(block * BLOCK, count)
+        rate = rbuf[block].astype(F32)[:8, :count].T[:, :1]
+        place = block * BLOCK + lax.broadcasted_iota(jnp.int32, (count, 1), 0)
+        weighted = rate * vbuf[rows, :].astype(F32)
+        target[rows, :] = jnp.where(place < bound, weighted, 0.0).astype(BF16)
     step = 384
     for part in range(HIGH // step):
         rows = pl.ds(part * step, step)
-        rate = jnp.sum(rates[rows, :].astype(F32) * pick, axis=1, keepdims=True)
-        place = part * step + lax.broadcasted_iota(jnp.int32, (step, 1), 0)
-        weighted = rate * vbuf[rows, :].astype(F32)
-        target[rows, :] = jnp.where(place < bound, weighted, 0.0).astype(BF16)
         k_rows = kbuf[rows, :]
         t_rows = target[rows, :]
         for tile in range(HID // 256):
@@ -171,11 +322,15 @@
         aim = jnp.sqrt(jnp.sum(wide * wide, axis=1, keepdims=True) + norm_epsilon)
         actual = jnp.sqrt(jnp.sum(moved * moved, axis=1, keepdims=True) + norm_epsilon)
         new_down[:, rows] = (moved * (aim / actual)).astype(BF16).T
-
-
-def fast_update(scalars, k_item, v_item, rates, gate_start, up_start, down_start):
+    stores = Fetcher(out_sems)
+    stores(new_gate, gate_out)
+    stores(new_up, up_out)
+    stores(new_down, down_out)
+    stores.wait()
+
+
+def fast_update(bounds, owns, others, starts):
     hbm = pl.BlockSpec(memory_space=pltpu.HBM)
-    vmem = pl.BlockSpec(memory_space=pltpu.VMEM)
     return pl.pallas_call(
         update_kernel,
         name="fast_update",
@@ -184,11 +339,15 @@
             jax.ShapeDtypeStruct((FDIM, HID), BF16),
             jax.ShapeDtypeStruct((HID, FDIM), BF16),
         ),
-        in_specs=[pl.BlockSpec(memory_space=pltpu.SMEM), hbm, hbm, vmem, hbm, hbm, hbm],
-        out_specs=(vmem, vmem, vmem),
+        in_specs=[pl.BlockSpec(memory_space=pltpu.SMEM)] + [hbm] * 11,
+        out_specs=(hbm, hbm, hbm),
         scratch_shapes=[
+            pltpu.VMEM((FDIM, HID), BF16),
+            pltpu.VMEM((FDIM, HID), BF16),
+            pltpu.VMEM((HID, FDIM), BF16),
             pltpu.VMEM((HIGH, FDIM), BF16),
             pltpu.VMEM((HIGH, FDIM), BF16),
+            pltpu.VMEM((CHIPS + 1, 16, FDIM), BF16),
             pltpu.VMEM((FDIM, HID), BF16),
             pltpu.VMEM((FDIM, HID), BF16),
             pltpu.VMEM((HID, FDIM), BF16),
@@ -202,30 +361,41 @@
             pltpu.VMEM((3, FDIM, HID), F32),
             pltpu.VMEM((3, FDIM, HID), BF16),
             pltpu.VMEM((6, FDIM, FDIM), BF16),
-            pltpu.SemaphoreType.DMA((13,)),
+            pltpu.SemaphoreType.DMA((18,)),
+            pltpu.SemaphoreType.DMA((3,)),
         ],
-        compiler_params=pltpu.CompilerParams(vmem_limit_bytes=48 * 1024 * 1024),
+        compiler_params=pltpu.CompilerParams(vmem_limit_bytes=VMEM_LIMIT),
         cost_estimate=pl.CostEstimate(
             flops=20_000_000_000, bytes_accessed=12_000_000, transcendentals=1_200_000
         ),
-    )(scalars, k_item, v_item, rates, gate_start, up_start, down_start)
+    )(bounds, *owns, *others, *starts)
 
 
 def apply_kernel(
     chunk,
-    scalars,
-    q_hbm,
-    k_hbm,
-    v_hbm,
-    hk_hbm,
-    hv_hbm,
+    bounds,
+    own_q,
+    other_q,
+    q1,
+    q2,
+    q3,
+    own0,
+    own1,
+    own2,
+    own3,
+    other0,
+    other1,
+    other2,
+    other3,
+    halo,
     gate_hbm,
     up_hbm,
     down_hbm,
-    new_gate,
-    new_up,
-    new_down,
-    gain,
+    gate_new,
+    up_new,
+    down_new,
+    gain_hbm,
+    out_hbm,
     out,
     qc,
     kbuf,
@@ -233,41 +403,63 @@
     wg,
     wu,
     wd,
+    new_gate,
+    new_up,
+    new_down,
+    gain,
     hid,
     raw,
     before,
     fast,
     sems,
+    out_sem,
 ):
-    bound = scalars[0]
-    parity = scalars[1]
-    sequence = scalars[2]
-    owned = scalars[3]
-    copies = []
-
-    def fetch(src, dst):
-        copy = pltpu.make_async_copy(src, dst, sems.at[len(copies)])
-        copy.start()
-        copies.append(copy)
-
-    for block in range(SPLIT):
-        src = pl.ds(place_of(block) * BLOCK + chunk * HALF, HALF)
-        fetch(q_hbm.at[src], qc.at[pl.ds(block * HALF, HALF)])
+    column, parity, sequence = position()
+    bound = bounds[sequence]
+    owned = 2 * column + parity
+    fetch = Fetcher(sems)
+
+    def q_rows_of(core, source):
+        return qc.at[pl.ds(pl.multiple_of((core * CHIPS + source) * HALF, HALF), HALF)]
+
+    def sender(slot):
+        return lax.rem(column + CHIPS - slot, CHIPS)
+
     fetch(gate_hbm.at[parity], wg)
     fetch(up_hbm.at[parity], wu)
+    q_src = pl.ds(chunk * HALF, HALF)
+    fetch(own_q.at[0, q_src], q_rows_of(parity, column))
+    fetch(other_q.at[0, q_src], q_rows_of(1 - parity, column))
+    for slot, array in ((1, q1), (2, q2), (3, q3)):
+        fetch(array.at[q_src], q_rows_of(parity, sender(slot)))
+        fetch(array.at[pl.ds(BLOCK + chunk * HALF, HALF)], q_rows_of(1 - parity, sender(slot)))
+    early = len(fetch.copies)
     fetch(down_hbm.at[parity], wd)
-    first = len(copies)
-    fetch(hk_hbm, kbuf.at[pl.ds(0, WINDOW)])
-    fetch(hv_hbm, vbuf.at[pl.ds(0, WINDOW)])
-    for block in range(SPLIT):
-        src = pl.ds(place_of(block) * BLOCK, BLOCK)
-        dst = pl.ds(WINDOW + block * BLOCK, BLOCK)
-        fetch(k_hbm.at[src], kbuf.at[dst])
-        fetch(v_hbm.at[src], vbuf.at[dst])
-    for copy in copies[:first]:
-        copy.wait()
-
-    def swiglu(rows, gate, up, down, store):
+    downs = len(fetch.copies)
+    fetch(gate_new, new_gate)
+    fetch(up_new, new_up)
+    fetch(down_new, new_down)
+    fetch(gain_hbm, gain)
+    first = len(fetch.copies)
+    fetch.wait(0, early)
+    for which, buf in ((0, kbuf), (1, vbuf)):
+        rows = pl.ds(which * BLOCK, BLOCK)
+
+        def rows_at(core, source, buf=buf):
+            start = WINDOW + (core * CHIPS + source) * BLOCK
+            return buf.at[pl.ds(pl.multiple_of(start, BLOCK), BLOCK)]
+
+        fetch(halo.at[pl.ds(which * WINDOW, WINDOW)], buf.at[pl.ds(0, WINDOW)])
+        for slot, own, other in (
+            (0, own0, other0),
+            (1, own1, other1),
+            (2, own2, other2),
+            (3, own3, other3),
+        ):
+            fetch(own.at[rows], rows_at(parity, sender(slot)))
+            fetch(other.at[rows], rows_at(1 - parity, sender(slot)))
+
+    def swiglu(rows, gate, up, down, store, ready):
         in_rows = qc[rows, :]
         for tile in range(HID // 256):
             cols = pl.ds(tile * 256, 256)
@@ -276,6 +468,7 @@
             hid[pl.ds(0, rows.size), cols] = (
                 pre_gate / (1.0 + jnp.exp(-pre_gate)) * pre_up
             ).astype(BF16)
+        ready()
         store(dot(hid[pl.ds(0, rows.size), :], down[...]))
 
     edge = 4 if chunk == 0 else 3
@@ -289,8 +482,9 @@
     def store_new(value):
         raw[new_rows, :] = value
 
-    swiglu(old_rows, wg, wu, wd, store_old)
-    swiglu(new_rows, new_gate, new_up, new_down, store_new)
+    swiglu(old_rows, wg, wu, wd, store_old, lambda: fetch.wait(early, downs))
+    fetch.wait(downs, first)
+    swiglu(new_rows, new_gate, new_up, new_down, store_new, lambda: None)
     mid = pl.ds(edge * HALF, HALF)
     place = edge * BLOCK + chunk * HALF + lax.broadcasted_iota(jnp.int32, (HALF, 1), 0)
     raw[mid, :] = jnp.where(place < bound, before[...], raw[mid, :])
@@ -300,8 +494,7 @@
         value = raw[rows, :]
         root = jnp.sqrt(jnp.mean(value * value, axis=1, keepdims=True) + rms_epsilon)
         fast[rows, :] = (value / root * gain_row).astype(BF16)
-    for copy in copies[first:]:
-        copy.wait()
+    fetch.wait(first)
 
     row_iota = lax.broadcasted_iota(jnp.int32, (HALF, HALF), 0)
     col_iota = lax.broadcasted_iota(jnp.int32, (HALF, HALF), 1)
@@ -341,79 +534,114 @@
 
     lax.fori_loop(0, 2, edge_body, 0)
     lax.fori_loop(2, SPLIT, main_body, 0)
-
-
-def apply_chunk(
-    chunk, scalars, q_item, k_item, v_item, halo_k, halo_v, starts, news, gain
-):
+    copy = pltpu.make_async_copy(out, out_hbm, out_sem)
+    copy.start()
+    copy.wait()
+
+
+def apply_chunk(chunk, bounds, local_q, q_parts, owns, others, halo, starts, news, gain):
     hbm = pl.BlockSpec(memory_space=pltpu.HBM)
-    vmem = pl.BlockSpec(memory_space=pltpu.VMEM)
     rows = SPLIT * HALF
     return pl.pallas_call(
         functools.partial(apply_kernel, chunk),
         name="apply_attend",
         out_shape=jax.ShapeDtypeStruct((rows, FDIM), BF16),
-        in_specs=[pl.BlockSpec(memory_space=pltpu.SMEM)] + [hbm] * 8 + [vmem] * 4,
-        out_specs=vmem,
+        in_specs=[pl.BlockSpec(memory_space=pltpu.SMEM)] + [hbm] * 21,
+        out_specs=hbm,
         scratch_shapes=[
+            pltpu.VMEM((rows, FDIM), BF16),
             pltpu.VMEM((rows, FDIM), BF16),
             pltpu.VMEM((WINDOW + LEN, FDIM), BF16),
             pltpu.VMEM((WINDOW + LEN, FDIM), BF16),
             pltpu.VMEM((FDIM, HID), BF16),
             pltpu.VMEM((FDIM, HID), BF16),
             pltpu.VMEM((HID, FDIM), BF16),
+            pltpu.VMEM((FDIM, HID), BF16),
+            pltpu.VMEM((FDIM, HID), BF16),
+            pltpu.VMEM((HID, FDIM), BF16),
+            pltpu.VMEM((SPLIT, FDIM), F32),
             pltpu.VMEM((5 * HALF, HID), BF16),
             pltpu.VMEM((rows, FDIM), F32),
             pltpu.VMEM((HALF, FDIM), F32),
             pltpu.VMEM((rows, FDIM), BF16),
-            pltpu.SemaphoreType.DMA((29,)),
+            pltpu.SemaphoreType.DMA((33,)),
+            pltpu.SemaphoreType.DMA,
         ],
-        compiler_params=pltpu.CompilerParams(vmem_limit_bytes=40 * 1024 * 1024),
+        compiler_params=pltpu.CompilerParams(vmem_limit_bytes=VMEM_LIMIT),
         cost_estimate=pl.CostEstimate(
             flops=8_000_000_000, bytes_accessed=14_000_000, transcendentals=4_000_000
         ),
-    )(scalars, q_item, k_item, v_item, halo_k, halo_v, *starts, *news, gain)
+    )(bounds, *local_q, *q_parts, *owns, *others, halo, *starts, *news, gain)
 
 
 def body(queries, keys, values, token_rates, gate_start, up_start, down_start, norm_gain, bounds):
     shards = lax.axis_size("tok") * lax.axis_size("head")
     column = lax.axis_index("head")
     parity = lax.axis_index("tok") % 2
-    owned = 2 * column + parity
-    sequence = lax.axis_index("tok") // 2
     groups = [
-        [s * SPLIT + (i % 2) * 4 + i // 2 for i in range(SPLIT)] for s in range(shards // SPLIT)
+        [s * SPLIT + place for place in sorted(range(SPLIT), key=lambda b: (b % CHIPS, b // CHIPS))]
+        for s in range(shards // SPLIT)
     ]
-    plain_groups = [[s * SPLIT + i for i in range(SPLIT)] for s in range(shards // SPLIT)]
-    span_bound = lax.dynamic_index_in_dim(bounds, sequence, 0, keepdims=False)
-    scalars = jnp.stack([span_bound, parity, sequence, owned]).astype(jnp.int32)
-
-    def spread(array):
-        return lax.all_to_all(
-            array, AXES, split_axis=1, concat_axis=0, tiled=True, axis_index_groups=groups
+    tok_count = lax.axis_size("tok")
+
+    def across_core(array):
+        return lax.ppermute(array, "tok", [(i, i ^ 1) for i in range(tok_count)])
+
+    def along(array, slot):
+        return lax.ppermute(array, "head", [(i, (i + slot) % CHIPS) for i in range(CHIPS)])
+
+    def next_segment(array):
+        return lax.ppermute(array, "tok", [(i, i + 2) for i in range(tok_count - 2)])
+
+    order = (1, 3, 2)
+    own_kv, swap_kv = pack_kv(keys, values, token_rates.T)
+    other_kv = across_core(swap_kv)
+    owns, others = [own_kv[0]] * CHIPS, [other_kv[0]] * CHIPS
+    for slot in order:
+        owns[slot] = along(own_kv[slot], slot)
+    queries, owns[0] = lax.optimization_barrier((queries, owns[0]))
+    own_q, swap_q = pack_q(queries)
+    other_q = across_core(swap_q)
+    for slot in order:
+        others[slot] = along(other_kv[slot], slot)
+    q_parts = [None] * CHIPS
+    for slot in order:
+        part = jnp.concatenate([own_q[slot], other_q[slot]], axis=0)
+        others[slot], part = lax.optimization_barrier((others[slot], part))
+        q_parts[slot] = along(part, slot)
+
+    first_core = parity == 0
+
+    def tail(source):
+        value = jnp.where(first_core, others[0], owns[0])
+        for slot in order:
+            here = jnp.where(first_core, others[slot], owns[slot])
+            value = jnp.where(column == (source + slot) % CHIPS, here, value)
+        return value
+
+    tails = [tail(source) for source in (2, 3)]
+    halo = next_segment(
+        jnp.concatenate(
+            [t[part * BLOCK : (part + 1) * BLOCK] for part in range(2) for t in tails], axis=0
         )
-
-    def halo(item):
-        tail = jnp.concatenate(
-            [item[place_of(b) * BLOCK : (place_of(b) + 1) * BLOCK] for b in (6, 7)], axis=0
-        )
-        count = lax.axis_size("tok")
-        return lax.ppermute(tail, "tok", [(i, i + 2) for i in range(count - 2)])
-
-    rates = lax.all_gather(token_rates, AXES, axis=0, tiled=True, axis_index_groups=plain_groups)
-    keys, rates = lax.optimization_barrier((keys, rates))
-    k_item = spread(keys)
-    v_item = spread(values)
-    halo_k = halo(k_item)
-    halo_v = halo(v_item)
-    q_item = spread(queries)
+    )
+
     starts = (gate_start, up_start, down_start)
-    news = fast_update(scalars, k_item, v_item, rates, *starts)
+    news = fast_update(bounds, owns, others, starts)
     gain = norm_gain.reshape(-1, FDIM)
     returned = []
     for chunk in range(2):
         out = apply_chunk(
-            chunk, scalars, q_item, k_item, v_item, halo_k, halo_v, starts, news, gain
+            chunk,
+            bounds,
+            (own_q, other_q),
+            q_parts[1:],
+            owns,
+            others,
+            halo,
+            starts,
+            news,
+            gain,
         )
         returned.append(
             lax.all_to_all(

time: 212 us -> 168 us (0.79)
  local copies, waits for them, and re-layouts: 34.2 us -> 4.54 us
  blocking collectives: 24.7 us -> 0 us
  Pallas kernels: 65.8 us -> 76.5 us
  waiting for transfers between devices: 49.8 us -> 44.6 us
  starting transfers between devices: 32.2 us -> 35.9 us
    all_to_all x3 -> x0, waiting for transfers between devices: 36 us -> none  [spread(): lax.all_to_all(array, AXES, split_axis=1, concat_axis=0, tiled=True, axis...]
    ppermute x2 -> x12, waiting for transfers between devices: 0.01 us -> 29.7 us  [the longest x9 28.7 us: along(): lax.ppermute(array, 'head', [(i, (i + slot) % CHIPS) for i in range(CHIPS)])]
    all_gather x1 -> x0, blocking collectives: 24.7 us -> none  [body(): lax.all_gather(token_rates, AXES, axis=0, tiled=True, axis_index_groups=p...]
    ppermute x2 -> x12, starting transfers between devices: 7.97 us -> 25.6 us  [the longest x9 20.2 us: along(): lax.ppermute(array, 'head', [(i, (i + slot) % CHIPS) for i in range(CHIPS)])]
    unnamed x28 -> x12, local copies, waits for them, and re-layouts: 18.4 us -> 0.99 us
    all_to_all x3 -> x0, starting transfers between devices: 14.3 us -> none  [spread(): lax.all_to_all(array, AXES, split_axis=1, concat_axis=0, tiled=True, axis...]
    all_to_all x3 -> x0, local copies, waits for them, and re-layouts: 9.42 us -> none  [spread(): lax.all_to_all(array, AXES, split_axis=1, concat_axis=0, tiled=True, axis...]
    pallas_call x0 -> x2, Pallas kernels: none -> 7.56 us  [the longest x1 4.58 us: pack_kv(): pl.pallas_call(pack_kv_kernel, name='pack_kv', out_shape=(shape,) * CHIPS...]
  transfers between devices with their start and end apart: 7 -> 14, of which waited for: 3 -> 5; matrix products, arithmetic and copies ran while one was open for 8% -> 5% of each run, Pallas kernels for 22% -> 31%
where the time goes in v1:
time: 168 us
  Pallas kernels  76.5 us (46%)
  waiting for transfers between devices  44.6 us (27%)
  starting transfers between devices  35.9 us (21%)
  other arithmetic  5.75 us (3%)
  local copies, waits for them, and re-layouts  4.54 us (3%)
    pallas_call x2, Pallas kernels, apply_chunk(): pl.pallas_call(functools.partial(apply_kernel, chunk), name='apply_attend...  38.8 us
    pallas_call x1, Pallas kernels, fast_update(): pl.pallas_call(update_kernel, name='fast_update', out_shape=(jax.ShapeDty...  30.2 us
    ppermute x9, waiting for transfers between devices, along(): lax.ppermute(array, 'head', [(i, (i + slot) % CHIPS) for i in range(CHIPS)])  28.7 us
    ppermute x9, starting transfers between devices, along(): lax.ppermute(array, 'head', [(i, (i + slot) % CHIPS) for i in range(CHIPS)])  20.2 us
    all_to_all x2, waiting for transfers between devices, body(): lax.all_to_all(out, AXES, split_axis=0, concat_axis=1, tiled=True, axis_i...  15 us
    all_to_all x2, starting transfers between devices, body(): lax.all_to_all(out, AXES, split_axis=0, concat_axis=1, tiled=True, axis_i...  10.3 us
    pallas_call x1, Pallas kernels, pack_kv(): pl.pallas_call(pack_kv_kernel, name='pack_kv', out_shape=(shape,) * CHIPS...  4.58 us
    ppermute x1, starting transfers between devices, next_segment(): lax.ppermute(array, 'tok', [(i, i + 2) for i in range(tok_count - 2)])  3.79 us
  transfers between devices with their start and end apart: 14, of which 5 were waited for; matrix products, arithmetic and copies ran while one was open for 5% of the time, Pallas kernels for 31%

profile of v1, /device:TPU:1, one launch (start us, length us, event | category | flops | bytes accessed | tf_op | source)
XLA Modules:
  0.0 167.6 jit_solution(17701399639109535317)
XLA Ops:
  0.0 4.6 %pack_kv.1 = (bf16[528,512]{1,0:T(8,128)(2,1)}, bf16[528,512]{1,0:T(8,128)(2,1)}, bf16[528,512]{1,0:T(8,128)(2,1)}, bf16[528,512]{1,0:T(8,128)(2,1)}, bf16[4,528,512]{2,1,0:T(8,128)(2,1)}) custom-call(bf16[256,4096]{1,0:T(8,128)(2,1)} %keys.1, bf16[256,4096]{1,0:T(8,128)(2,1)} %values.1, bf16[8,256]{1,0:T(8,128)(2,1)} %bitcast.39), custom_call_target="tpu_custom_call" | custom-call | bytes 16000000 | tf_op jit(solution)/shard_map/pack_kv/pallas_call | solution.py:114
  4.6 1.5 collective-permute-start.1
  6.1 3.0 %pack_q.1 = (bf16[4,256,512]{2,1,0:T(8,128)(2,1)}, bf16[4,256,512]{2,1,0:T(8,128)(2,1)}) custom-call(bf16[256,4096]{1,0:T(8,128)(2,1)} %queries), custom_call_target="tpu_custom_call" | custom-call | bytes 8000000 | tf_op jit(solution)/shard_map/pack_q/pallas_call | solution.py:151
  9.1 0.0 copy-start.4
  9.1 0.0 copy-start
  9.1 0.1 collective-permute-start
  9.2 1.0 collective-permute-done.1
  10.2 1.4 slice_bitcast_fusion
  11.6 2.6 %collective-permute-start.6 = (bf16[528,512]{1,0:T(8,128)(2,1)}, bf16[528,512]{1,0:T(8,128)(2,1)}, u32[]{:S(2)}, u32[]{:S(2)}) collective-permute-start(bf16[528,512]{1,0:T(8,128)(2,1)} %get-tuple-element.44), channel_id=1, source_target_pairs={{0,3},{1,0},{2,1},{3,2},{4,7},{5,4},{6,5},{7,6},{8,11},{9,8},{10,9... | collective-permute-start | bytes 1622024 | tf_op jit(solution)/shard_map/ppermute | solution.py:591
  14.1 0.0 collective-permute-start.8
  14.1 1.7 %collective-permute-start.9 = (bf16[528,512]{1,0:T(8,128)(2,1)}, bf16[528,512]{1,0:T(8,128)(2,1)}, u32[]{:S(2)}, u32[]{:S(2)}) collective-permute-start(bf16[528,512]{1,0:T(8,128)(2,1)} %get-tuple-element.33), channel_id=1, source_target_pairs={{0,2},{1,3},{2,0},{3,1},{4,6},{5,7},{6,4},{7,5},{8,10},{9,11},{10,... | collective-permute-start | bytes 1622024 | tf_op jit(solution)/shard_map/ppermute | solution.py:591
  15.9 0.9 collective-permute-start.10
  16.8 0.6 reshape.9.gain_hbm
  17.4 0.1 slice_bitcast_fusion.7
  17.5 0.0 collective-permute-done.other_q
  17.5 2.4 %collective-permute-start.4 = (bf16[528,512]{1,0:T(8,128)(2,1)}, bf16[528,512]{1,0:T(8,128)(2,1)S(1)}, u32[]{:S(2)}, u32[]{:S(2)}) collective-permute-start(bf16[528,512]{1,0:T(8,128)(2,1)} %get-tuple-element.45), channel_id=1, source_target_pairs={{0,2},{1,3},{2,0},{3,1},{4,6},{5,7},{6,4},{7,5},{8,10},{9,11},{10,... | collective-permute-start | bytes 1622024 | tf_op jit(solution)/shard_map/ppermute | solution.py:591
  19.9 16.6 %collective-permute-done.6.other3 = bf16[528,512]{1,0:T(8,128)(2,1)} collective-permute-done((bf16[528,512]{1,0:T(8,128)(2,1)}, bf16[528,512]{1,0:T(8,128)(2,1)}, u32[]{:S(2)}, u32[]{:S(2)}) %collective-permute-start.6) | collective-permute-done | bytes 540704 | tf_op jit(solution)/shard_map/ppermute | solution.py:591
  36.6 0.0 collective-permute-start.2
  36.6 1.2 slice_bitcast_fusion.4
  37.8 0.8 pad_maximum_fusion.4
  38.6 0.8 pad_maximum_fusion.3
  39.4 0.8 pad_maximum_fusion.2
  40.3 10.7 %collective-permute-done.4.other2 = bf16[528,512]{1,0:T(8,128)(2,1)S(1)} collective-permute-done((bf16[528,512]{1,0:T(8,128)(2,1)}, bf16[528,512]{1,0:T(8,128)(2,1)S(1)}, u32[]{:S(2)}, u32[]{:S(2)}) %collective-permute-start.4) | collective-permute-done | bytes 540704 | tf_op jit(solution)/shard_map/ppermute | solution.py:591
  51.0 11.5 %collective-permute-start.7 = (bf16[512,512]{1,0:T(8,128)(2,1)}, bf16[512,512]{1,0:T(8,128)(2,1)}, u32[]{:S(2)}, u32[]{:S(2)}) collective-permute-start(bf16[512,512]{1,0:T(8,128)(2,1)} %pad_maximum_fusion.4), channel_id=1, source_target_pairs={{0,3},{1,0},{2,1},{3,2},{4,7},{5,4},{6,5},{7,6},{8,11},{9,8},{10,9... | collective-permute-start | bytes 1572872 | tf_op jit(solution)/shard_map/ppermute | solution.py:591
  62.5 1.3 collective-permute-done.2.other1
  63.8 1.0 collective-permute-start.5
  64.8 0.0 collective-permute-done.8.own1
  64.8 0.0 collective-permute-start.3
  64.8 0.0 collective-permute-done.9.own2
  64.8 0.0 collective-permute-done.10.own3
  64.9 1.6 select_select_fusion.1
  66.5 0.1 fusion
  66.6 0.1 pad_maximum_fusion.1
  66.7 3.8 %collective-permute-start.11 = (bf16[1024,512]{1,0:T(8,128)(2,1)S(1)}, bf16[1024,512]{1,0:T(8,128)(2,1)S(1)}, u32[]{:S(2)}, u32[]{:S(2)}) collective-permute-start(bf16[1024,512]{1,0:T(8,128)(2,1)S(1)} %pad_maximum_fusion.1), channel_id=1, source_target_pairs={{0,8},{4,12},{8,16},{12,20},{16,24},{20,28},{24,32},{28,36},{32,40... | collective-permute-start | bytes 3145736 | tf_op jit(solution)/shard_map/ppermute | solution.py:594
  70.5 30.2 %fast_update.1 = (bf16[512,1024]{1,0:T(8,128)(2,1)}, bf16[512,1024]{1,0:T(8,128)(2,1)}, bf16[1024,512]{1,0:T(8,128)(2,1)}) custom-call(s32[16]{0:T(128)} %bounds.5, bf16[528,512]{1,0:T(8,128)(2,1)} %get-tuple-element.31.own0, bf16[528,512]{1,0:T(8,128)(2,1)} %collective-permute-done.8.own1, bf16[528,512]{1,0:T(8,128)(2,1)} %collective-permute-done.9.own2, ...), custom_call_target="tpu_custom_call" | custom-call | flops 20000000000 | bytes 12000000 | tf_op jit(solution)/shard_map/fast_update/pallas_call | solution.py:334
  100.6 0.0 collective-permute-done.7.q3
  100.6 0.0 collective-permute-done.5.q2
  100.7 0.0 collective-permute-done.3.q1
  100.7 0.0 collective-permute-done.11.halo
  100.7 1.0 copy-done.5
  101.7 19.4 %apply_attend.3 = bf16[1024,512]{1,0:T(8,128)(2,1)} custom-call(s32[16]{0:T(128)} %bounds.5, bf16[4,256,512]{2,1,0:T(8,128)(2,1)} %get-tuple-element.25.own_q, bf16[4,256,512]{2,1,0:T(8,128)(2,1)} %collective-permute-done.other_q, bf16[512,512]{1,0:T(8,128)(2,1)} %collective-permute-done.3.q1, bf16[512,512]{1,0:T(8,128)(2,1)} %collective-permute-done.5.q2, ...), custom_call_target="tpu_custom_call" | custom-call | flops 8000000000 | bytes 14000000 | tf_op jit(solution)/shard_map/apply_attend/pallas_call | solution.py:545
  121.1 5.5 %all-to-all-start.1 = ((bf16[8,128,512]{2,1,0:T(8,128)(2,1)}), bf16[8,128,512]{2,1,0:T(8,128)(2,1)S(1)}, u32[]{:S(2)}, u32[]{:S(2)}) async-start(bf16[8,128,512]{2,1,0:T(8,128)(2,1)} %bitcast.38), calls=%async_computation.1 | async-start | bytes 2097152 | tf_op jit(solution)/shard_map/all_to_all | solution.py:647
  126.6 19.4 %apply_attend.2 = bf16[1024,512]{1,0:T(8,128)(2,1)} custom-call(s32[16]{0:T(128)} %bounds.5, bf16[4,256,512]{2,1,0:T(8,128)(2,1)} %get-tuple-element.25.own_q, bf16[4,256,512]{2,1,0:T(8,128)(2,1)} %collective-permute-done.other_q, bf16[512,512]{1,0:T(8,128)(2,1)} %collective-permute-done.3.q1, bf16[512,512]{1,0:T(8,128)(2,1)} %collective-permute-done.5.q2, ...), custom_call_target="tpu_custom_call" | custom-call | flops 8000000000 | bytes 14000000 | tf_op jit(solution)/shard_map/apply_attend/pallas_call | solution.py:545
  146.0 4.8 %all-to-all-start = ((bf16[8,128,512]{2,1,0:T(8,128)(2,1)}), bf16[8,128,512]{2,1,0:T(8,128)(2,1)S(1)}, u32[]{:S(2)}, u32[]{:S(2)}) async-start(bf16[8,128,512]{2,1,0:T(8,128)(2,1)} %bitcast.37), calls=%async_computation | async-start | bytes 2097152 | tf_op jit(solution)/shard_map/all_to_all | solution.py:647
  150.8 0.1 copy.13
  150.9 15.0 %all-to-all-done = bf16[8,128,512]{2,1,0:T(8,128)(2,1)S(1)} async-done(((bf16[8,128,512]{2,1,0:T(8,128)(2,1)}), bf16[8,128,512]{2,1,0:T(8,128)(2,1)S(1)}, u32[]{:S(2)}, u32[]{:S(2)}) %all-to-all-start) | async-done | bytes 1048608 | tf_op jit(solution)/shard_map/all_to_all | solution.py:647
  165.9 0.1 copy.12
  166.0 1.5 pad_maximum_fusion
  (10 shorter events, 0.0 us)
Async XLA Ops:
  4.6 5.6 %collective-permute-start.1 = (bf16[4,528,512]{2,1,0:T(8,128)(2,1)}, bf16[4,528,512]{2,1,0:T(8,128)(2,1)S(1)}, u32[]{:S(2)}, u32[]{:S(2)}) collective-permute-start(bf16[4,528,512]{2,1,0:T(8,128)(2,1)} %get-tuple-element.27), channel_id=1, source_target_pairs={{0,4},{4,0},{8,12},{12,8},{16,20},{20,16},{24,28},{28,24},{32,36},... | collective-permute-start | bytes 6488072 | tf_op jit(solution)/shard_map/ppermute | solution.py:588
  9.1 7.7 %copy-start.4 = (f32[4096]{0:T(1024)S(1)}, f32[4096]{0:T(1024)}, u32[]{:S(2)}) copy-start(f32[4096]{0:T(1024)} %param.16) | copy-start | bytes 49156
  9.1 8.3 %copy-start = (bf16[4,256,512]{2,1,0:T(8,128)(2,1)S(1)}, bf16[4,256,512]{2,1,0:T(8,128)(2,1)}, u32[]{:S(2)}) copy-start(bf16[4,256,512]{2,1,0:T(8,128)(2,1)} %get-tuple-element.25.own_q) | copy-start | bytes 3145732
  9.1 8.4 %collective-permute-start = (bf16[4,256,512]{2,1,0:T(8,128)(2,1)}, bf16[4,256,512]{2,1,0:T(8,128)(2,1)}, u32[]{:S(2)}, u32[]{:S(2)}) collective-permute-start(bf16[4,256,512]{2,1,0:T(8,128)(2,1)} %get-tuple-element.26), channel_id=1, source_target_pairs={{0,4},{4,0},{8,12},{12,8},{16,20},{20,16},{24,28},{28,24},{32,36},... | collective-permute-start | bytes 3145736 | tf_op jit(solution)/shard_map/ppermute | solution.py:588
  11.6 25.0 %collective-permute-start.6 = (bf16[528,512]{1,0:T(8,128)(2,1)}, bf16[528,512]{1,0:T(8,128)(2,1)}, u32[]{:S(2)}, u32[]{:S(2)}) collective-permute-start(bf16[528,512]{1,0:T(8,128)(2,1)} %get-tuple-element.44), channel_id=1, source_target_pairs={{0,3},{1,0},{2,1},{3,2},{4,7},{5,4},{6,5},{7,6},{8,11},{9,8},{10,9... | collective-permute-start | bytes 1622024 | tf_op jit(solution)/shard_map/ppermute | solution.py:591
  14.1 50.7 %collective-permute-start.8 = (bf16[528,512]{1,0:T(8,128)(2,1)}, bf16[528,512]{1,0:T(8,128)(2,1)}, u32[]{:S(2)}, u32[]{:S(2)}) collective-permute-start(bf16[528,512]{1,0:T(8,128)(2,1)} %get-tuple-element.32), channel_id=1, source_target_pairs={{0,1},{1,2},{2,3},{3,0},{4,5},{5,6},{6,7},{7,4},{8,9},{9,10},{10,1... | collective-permute-start | bytes 1622024 | tf_op jit(solution)/shard_map/ppermute | solution.py:591
  14.1 50.7 %collective-permute-start.9 = (bf16[528,512]{1,0:T(8,128)(2,1)}, bf16[528,512]{1,0:T(8,128)(2,1)}, u32[]{:S(2)}, u32[]{:S(2)}) collective-permute-start(bf16[528,512]{1,0:T(8,128)(2,1)} %get-tuple-element.33), channel_id=1, source_target_pairs={{0,2},{1,3},{2,0},{3,1},{4,6},{5,7},{6,4},{7,5},{8,10},{9,11},{10,... | collective-permute-start | bytes 1622024 | tf_op jit(solution)/shard_map/ppermute | solution.py:591
  15.9 49.0 %collective-permute-start.10 = (bf16[528,512]{1,0:T(8,128)(2,1)}, bf16[528,512]{1,0:T(8,128)(2,1)}, u32[]{:S(2)}, u32[]{:S(2)}) collective-permute-start(bf16[528,512]{1,0:T(8,128)(2,1)} %get-tuple-element.34), channel_id=1, source_target_pairs={{0,3},{1,0},{2,1},{3,2},{4,7},{5,4},{6,5},{7,6},{8,11},{9,8},{10,9... | collective-permute-start | bytes 1622024 | tf_op jit(solution)/shard_map/ppermute | solution.py:591
  17.5 33.5 %collective-permute-start.4 = (bf16[528,512]{1,0:T(8,128)(2,1)}, bf16[528,512]{1,0:T(8,128)(2,1)S(1)}, u32[]{:S(2)}, u32[]{:S(2)}) collective-permute-start(bf16[528,512]{1,0:T(8,128)(2,1)} %get-tuple-element.45), channel_id=1, source_target_pairs={{0,2},{1,3},{2,0},{3,1},{4,6},{5,7},{6,4},{7,5},{8,10},{9,11},{10,... | collective-permute-start | bytes 1622024 | tf_op jit(solution)/shard_map/ppermute | solution.py:591
  36.6 28.3 %copy-start.1 = (bf16[528,512]{1,0:T(8,128)(2,1)S(1)}, bf16[528,512]{1,0:T(8,128)(2,1)}, u32[]{:S(2)}) copy-start(bf16[528,512]{1,0:T(8,128)(2,1)} %get-tuple-element.31.own0) | copy-start | bytes 1622020
  36.6 27.3 %collective-permute-start.2 = (bf16[528,512]{1,0:T(8,128)(2,1)}, bf16[528,512]{1,0:T(8,128)(2,1)S(1)}, u32[]{:S(2)}, u32[]{:S(2)}) collective-permute-start(bf16[528,512]{1,0:T(8,128)(2,1)} %get-tuple-element.46), channel_id=1, source_target_pairs={{0,1},{1,2},{2,3},{3,0},{4,5},{5,6},{6,7},{7,4},{8,9},{9,10},{10,1... | collective-permute-start | bytes 1622024 | tf_op jit(solution)/shard_map/ppermute | solution.py:591
  51.0 15.5 %copy-start.2 = (bf16[528,512]{1,0:T(8,128)(2,1)}, bf16[528,512]{1,0:T(8,128)(2,1)S(1)}, u32[]{:S(2)}) copy-start(bf16[528,512]{1,0:T(8,128)(2,1)S(1)} %collective-permute-done.4.other2) | copy-start | bytes 1622020
  51.0 49.6 %collective-permute-start.7 = (bf16[512,512]{1,0:T(8,128)(2,1)}, bf16[512,512]{1,0:T(8,128)(2,1)}, u32[]{:S(2)}, u32[]{:S(2)}) collective-permute-start(bf16[512,512]{1,0:T(8,128)(2,1)} %pad_maximum_fusion.4), channel_id=1, source_target_pairs={{0,3},{1,0},{2,1},{3,2},{4,7},{5,4},{6,5},{7,6},{8,11},{9,8},{10,9... | collective-permute-start | bytes 1572872 | tf_op jit(solution)/shard_map/ppermute | solution.py:591
  63.8 2.7 %copy-start.3 = (bf16[528,512]{1,0:T(8,128)(2,1)}, bf16[528,512]{1,0:T(8,128)(2,1)S(1)}, u32[]{:S(2)}) copy-start(bf16[528,512]{1,0:T(8,128)(2,1)S(1)} %collective-permute-done.2.other1) | copy-start | bytes 1622020
  63.8 36.8 %collective-permute-start.5 = (bf16[512,512]{1,0:T(8,128)(2,1)}, bf16[512,512]{1,0:T(8,128)(2,1)}, u32[]{:S(2)}, u32[]{:S(2)}) collective-permute-start(bf16[512,512]{1,0:T(8,128)(2,1)} %pad_maximum_fusion.3), channel_id=1, source_target_pairs={{0,2},{1,3},{2,0},{3,1},{4,6},{5,7},{6,4},{7,5},{8,10},{9,11},{10,... | collective-permute-start | bytes 1572872 | tf_op jit(solution)/shard_map/ppermute | solution.py:591
  64.8 35.8 %collective-permute-start.3 = (bf16[512,512]{1,0:T(8,128)(2,1)}, bf16[512,512]{1,0:T(8,128)(2,1)}, u32[]{:S(2)}, u32[]{:S(2)}) collective-permute-start(bf16[512,512]{1,0:T(8,128)(2,1)} %pad_maximum_fusion.2), channel_id=1, source_target_pairs={{0,1},{1,2},{2,3},{3,0},{4,5},{5,6},{6,7},{7,4},{8,9},{9,10},{10,1... | collective-permute-start | bytes 1572872 | tf_op jit(solution)/shard_map/ppermute | solution.py:591
  66.7 34.0 %collective-permute-start.11 = (bf16[1024,512]{1,0:T(8,128)(2,1)S(1)}, bf16[1024,512]{1,0:T(8,128)(2,1)S(1)}, u32[]{:S(2)}, u32[]{:S(2)}) collective-permute-start(bf16[1024,512]{1,0:T(8,128)(2,1)S(1)} %pad_maximum_fusion.1), channel_id=1, source_target_pairs={{0,8},{4,12},{8,16},{12,20},{16,24},{20,28},{24,32},{28,36},{32,40... | collective-permute-start | bytes 3145736 | tf_op jit(solution)/shard_map/ppermute | solution.py:594
  100.7 1.0 copy-start.5
  121.1 24.9 %all-to-all-start.1 = ((bf16[8,128,512]{2,1,0:T(8,128)(2,1)}), bf16[8,128,512]{2,1,0:T(8,128)(2,1)S(1)}, u32[]{:S(2)}, u32[]{:S(2)}) async-start(bf16[8,128,512]{2,1,0:T(8,128)(2,1)} %bitcast.38), calls=%async_computation.1 | async-start | bytes 2097152 | tf_op jit(solution)/shard_map/all_to_all | solution.py:647
  146.0 19.9 %all-to-all-start = ((bf16[8,128,512]{2,1,0:T(8,128)(2,1)}), bf16[8,128,512]{2,1,0:T(8,128)(2,1)S(1)}, u32[]{:S(2)}, u32[]{:S(2)}) async-start(bf16[8,128,512]{2,1,0:T(8,128)(2,1)} %bitcast.37), calls=%async_computation | async-start | bytes 2097152 | tf_op jit(solution)/shard_map/all_to_all | solution.py:647

commit v2 on v1

--- a/solution.py
+++ b/solution.py
@@ -74,18 +74,16 @@
     return column, lax.rem(tok, 2), lax.div(tok, 2)
 
 
-def pack_kv_kernel(keys, values, rates, *rest):
-    outs = rest[: CHIPS + 1]
-    kbuf, vbuf, lines, in_sems, sems = rest[CHIPS + 1 :]
-
-    def out_at(index):
-        return outs[index] if index < CHIPS else outs[CHIPS].at[index - CHIPS]
-
+def pack_kernel(keys, values, queries, rates, *rest):
+    kv_outs = rest[: 2 * CHIPS]
+    q_out, q_swap = rest[2 * CHIPS : 2 * CHIPS + 2]
+    kbuf, vbuf, qbuf, lines, in_sems, sems = rest[2 * CHIPS + 2 :]
     column, parity, _ = position()
     load = Fetcher(in_sems)
     fetch = Fetcher(sems)
     load(keys, kbuf)
     load(values, vbuf)
+    load(queries, qbuf)
     turned = rates[...].astype(F32)
     place = lax.broadcasted_iota(jnp.int32, turned.shape, 0)
     targets = []
@@ -99,69 +97,42 @@
         lines[index, :, pl.ds(0, BLOCK)] = jnp.broadcast_to(line, (16, BLOCK)).astype(BF16)
         lines[index, :, pl.ds(BLOCK, FDIM - BLOCK)] = jnp.zeros((16, FDIM - BLOCK), BF16)
     for index, head in targets:
-        fetch(lines.at[index], out_at(index).at[pl.ds(RATE_ROW, 16)])
-    for part, buf in ((0, kbuf), (1, vbuf)):
+        fetch(lines.at[index], kv_outs[index].at[pl.ds(RATE_ROW, 16)])
+    for part, buf in ((0, kbuf), (1, vbuf), (2, qbuf)):
         load.wait(part, part + 1)
         for index, head in targets:
             cols = pl.ds(pl.multiple_of(head * FDIM, FDIM), FDIM)
-            fetch(buf.at[:, cols], out_at(index).at[pl.ds(part * BLOCK, BLOCK)])
+            if part < 2:
+                dst = kv_outs[index].at[pl.ds(part * BLOCK, BLOCK)]
+            else:
+                dst = (q_out, q_swap)[index // CHIPS].at[index % CHIPS]
+            fetch(buf.at[:, cols], dst)
     fetch.wait()
 
 
-def pack_kv(keys, values, rates):
+def pack(keys, values, queries, rates):
     hbm = pl.BlockSpec(memory_space=pltpu.HBM)
-    shape = jax.ShapeDtypeStruct((KV_ROWS, FDIM), BF16)
+    kv_shape = jax.ShapeDtypeStruct((KV_ROWS, FDIM), BF16)
+    q_shape = jax.ShapeDtypeStruct((CHIPS, BLOCK, FDIM), BF16)
+    width = CHIPS * 2 * FDIM
     outs = pl.pallas_call(
-        pack_kv_kernel,
-        name="pack_kv",
-        out_shape=(shape,) * CHIPS + (jax.ShapeDtypeStruct((CHIPS, KV_ROWS, FDIM), BF16),),
-        in_specs=[hbm, hbm, pl.BlockSpec(memory_space=pltpu.VMEM)],
-        out_specs=(hbm,) * (CHIPS + 1),
+        pack_kernel,
+        name="pack",
+        out_shape=(kv_shape,) * (2 * CHIPS) + (q_shape, q_shape),
+        in_specs=[hbm, hbm, hbm, pl.BlockSpec(memory_space=pltpu.VMEM)],
+        out_specs=(hbm,) * (2 * CHIPS + 2),
         scratch_shapes=[
-            pltpu.VMEM((BLOCK, CHIPS * 2 * FDIM), BF16),
-            pltpu.VMEM((BLOCK, CHIPS * 2 * FDIM), BF16),
+            pltpu.VMEM((BLOCK, width), BF16),
+            pltpu.VMEM((BLOCK, width), BF16),
+            pltpu.VMEM((BLOCK, width), BF16),
             pltpu.VMEM((2 * CHIPS, 16, FDIM), BF16),
-            pltpu.SemaphoreType.DMA((2,)),
-            pltpu.SemaphoreType.DMA((24,)),
+            pltpu.SemaphoreType.DMA((3,)),
+            pltpu.SemaphoreType.DMA((32,)),
         ],
         compiler_params=pltpu.CompilerParams(vmem_limit_bytes=VMEM_LIMIT),
-        cost_estimate=pl.CostEstimate(flops=0, bytes_accessed=16_000_000, transcendentals=0),
-    )(keys, values, rates)
-    return outs[:CHIPS], outs[CHIPS]
-
-
-def pack_q_kernel(queries, own, swap, qbuf, in_sems, sems):
-    column, parity, _ = position()
-    load = Fetcher(in_sems)
-    fetch = Fetcher(sems)
-    load(queries, qbuf)
-    load.wait()
-    for which in range(2):
-        core = parity if which == 0 else 1 - parity
-        for slot in range(CHIPS):
-            head = 2 * lax.rem(column + slot, CHIPS) + core
-            cols = pl.ds(pl.multiple_of(head * FDIM, FDIM), FDIM)
-            fetch(qbuf.at[:, cols], (own, swap)[which].at[slot])
-    fetch.wait()
-
-
-def pack_q(queries):
-    hbm = pl.BlockSpec(memory_space=pltpu.HBM)
-    shape = jax.ShapeDtypeStruct((CHIPS, BLOCK, FDIM), BF16)
-    return pl.pallas_call(
-        pack_q_kernel,
-        name="pack_q",
-        out_shape=(shape, shape),
-        in_specs=[hbm],
-        out_specs=(hbm, hbm),
-        scratch_shapes=[
-            pltpu.VMEM((BLOCK, CHIPS * 2 * FDIM), BF16),
-            pltpu.SemaphoreType.DMA((1,)),
-            pltpu.SemaphoreType.DMA((8,)),
-        ],
-        compiler_params=pltpu.CompilerParams(vmem_limit_bytes=VMEM_LIMIT),
-        cost_estimate=pl.CostEstimate(flops=0, bytes_accessed=8_000_000, transcendentals=0),
-    )(queries)
+        cost_estimate=pl.CostEstimate(flops=0, bytes_accessed=24_000_000, transcendentals=0),
+    )(keys, values, queries, rates)
+    return outs[:CHIPS], outs[CHIPS : 2 * CHIPS], *outs[2 * CHIPS :]
 
 
 def dot(a, b):
@@ -234,18 +205,20 @@
     def rows_at(buf):
         return lambda block: buf.at[pl.ds(pl.multiple_of(block * BLOCK, BLOCK), BLOCK)]
 
-    fetch(gate_hbm.at[parity], wg)
-    fetch(up_hbm.at[parity], wu)
+    fetch(down_hbm.at[parity], wd)
     low_part(pl.ds(0, BLOCK), rows_at(kbuf))
     top_part(pl.ds(0, HALF), kbuf.at[pl.ds(CHIPS * BLOCK, HALF)])
-    fetch(down_hbm.at[parity], wd)
     low_part(pl.ds(BLOCK, BLOCK), rows_at(vbuf))
     top_part(pl.ds(BLOCK, HALF), vbuf.at[pl.ds(CHIPS * BLOCK, HALF)])
     low_part(pl.ds(RATE_ROW, 16), lambda block: rbuf.at[block])
     top_part(pl.ds(RATE_ROW, 16), rbuf.at[CHIPS])
-    fetch.wait()
-
+    fetch(gate_hbm.at[parity], wg)
+    fetch(up_hbm.at[parity], wu)
+    fetch.wait(0, 1)
     wdt[...] = wd[...].T
+    fetch.wait(1, 6)
+    kt[...] = kbuf[...].T
+    fetch.wait(6, 16)
     for block in range(CHIPS + 1):
         count = min(BLOCK, HIGH - block * BLOCK)
         rows = pl.ds(block * BLOCK, count)
@@ -253,6 +226,8 @@
         place = block * BLOCK + lax.broadcasted_iota(jnp.int32, (count, 1), 0)
         weighted = rate * vbuf[rows, :].astype(F32)
         target[rows, :] = jnp.where(place < bound, weighted, 0.0).astype(BF16)
+    tt[...] = target[...].T
+    fetch.wait(16)
     step = 384
     for part in range(HIGH // step):
         rows = pl.ds(part * step, step)
@@ -269,8 +244,6 @@
             hid[rows, cols] = (act * pre_up).astype(BF16)
             dgate[rows, cols] = (back * pre_up * slope).astype(BF16)
             dup[rows, cols] = (back * act).astype(BF16)
-    kt[...] = kbuf[...].T
-    tt[...] = target[...].T
 
     for which, (left, right) in enumerate(((kt, dgate), (kt, dup), (tt, hid))):
         total = jnp.zeros((1, 256), F32)
@@ -307,7 +280,10 @@
 
     lax.fori_loop(0, NS_ITERS, iteration, 0)
 
-    for which, (start, out) in enumerate(((wg, new_gate), (wu, new_up))):
+    stores = Fetcher(out_sems)
+    for which, (start, out, target_hbm) in enumerate(
+        ((wg, new_gate, gate_out), (wu, new_up, up_out))
+    ):
         for tile in range(HID // 256):
             cols = pl.ds(tile * 256, 256)
             wide = start[:, cols].astype(F32)
@@ -315,16 +291,14 @@
             aim = jnp.sqrt(jnp.sum(wide * wide, axis=0, keepdims=True) + norm_epsilon)
             actual = jnp.sqrt(jnp.sum(moved * moved, axis=0, keepdims=True) + norm_epsilon)
             out[:, cols] = (moved * (aim / actual)).astype(BF16)
+        stores(out, target_hbm)
     for tile in range(FDIM // 128):
         rows = pl.ds(tile * 128, 128)
         wide = wdt[rows, :].astype(F32)
         moved = wide + xs[2, rows, :].astype(F32)
         aim = jnp.sqrt(jnp.sum(wide * wide, axis=1, keepdims=True) + norm_epsilon)
         actual = jnp.sqrt(jnp.sum(moved * moved, axis=1, keepdims=True) + norm_epsilon)
-        new_down[:, rows] = (moved * (aim / actual)).astype(BF16).T
-    stores = Fetcher(out_sems)
-    stores(new_gate, gate_out)
-    stores(new_up, up_out)
+        new_down[rows, :] = (moved * (aim / actual)).astype(BF16)
     stores(new_down, down_out)
     stores.wait()
 
@@ -337,14 +311,14 @@
         out_shape=(
             jax.ShapeDtypeStruct((FDIM, HID), BF16),
             jax.ShapeDtypeStruct((FDIM, HID), BF16),
-            jax.ShapeDtypeStruct((HID, FDIM), BF16),
+            jax.ShapeDtypeStruct((FDIM, HID), BF16),
         ),
         in_specs=[pl.BlockSpec(memory_space=pltpu.SMEM)] + [hbm] * 11,
         out_specs=(hbm, hbm, hbm),
         scratch_shapes=[
             pltpu.VMEM((FDIM, HID), BF16),
             pltpu.VMEM((FDIM, HID), BF16),
-            pltpu.VMEM((HID, FDIM), BF16),
+            pltpu.VMEM((FDIM, HID), BF16),
             pltpu.VMEM((HIGH, FDIM), BF16),
             pltpu.VMEM((HIGH, FDIM), BF16),
             pltpu.VMEM((CHIPS + 1, 16, FDIM), BF16),
@@ -413,6 +387,8 @@
     fast,
     sems,
     out_sem,
+    scores,
+    rounded,
 ):
     column, parity, sequence = position()
     bound = bounds[sequence]
@@ -459,7 +435,7 @@
             fetch(own.at[rows], rows_at(parity, sender(slot)))
             fetch(other.at[rows], rows_at(1 - parity, sender(slot)))
 
-    def swiglu(rows, gate, up, down, store, ready):
+    def swiglu(rows, gate, up, down, product, store, ready):
         in_rows = qc[rows, :]
         for tile in range(HID // 256):
             cols = pl.ds(tile * 256, 256)
@@ -469,7 +445,7 @@
                 pre_gate / (1.0 + jnp.exp(-pre_gate)) * pre_up
             ).astype(BF16)
         ready()
-        store(dot(hid[pl.ds(0, rows.size), :], down[...]))
+        store(product(hid[pl.ds(0, rows.size), :], down[...]))
 
     edge = 4 if chunk == 0 else 3
     old_rows = pl.ds(0, (edge + 1) * HALF)
@@ -482,9 +458,9 @@
     def store_new(value):
         raw[new_rows, :] = value
 
-    swiglu(old_rows, wg, wu, wd, store_old, lambda: fetch.wait(early, downs))
+    swiglu(old_rows, wg, wu, wd, dot, store_old, lambda: fetch.wait(early, downs))
     fetch.wait(downs, first)
-    swiglu(new_rows, new_gate, new_up, new_down, store_new, lambda: None)
+    swiglu(new_rows, new_gate, new_up, new_down, dot_nt, store_new, lambda: None)
     mid = pl.ds(edge * HALF, HALF)
     place = edge * BLOCK + chunk * HALF + lax.broadcasted_iota(jnp.int32, (HALF, 1), 0)
     raw[mid, :] = jnp.where(place < bound, before[...], raw[mid, :])
@@ -506,22 +482,30 @@
         q_rows = pl.ds(pl.multiple_of(block * HALF, HALF), HALF)
         o_rows = pl.ds(pl.multiple_of(place_of(block) * HALF, HALF), HALF)
         keys = pl.ds(base, WINDOW + HALF)
-        for head in range(FDIM // AHD):
+        heads = range(FDIM // AHD)
+        for head in heads:
             cols = pl.ds(head * AHD, AHD)
-            scores = dot_nt(qc[q_rows, cols], kbuf[keys, cols])
-            parts = [scores[:, i * HALF : (i + 1) * HALF] for i in range(5)]
+            scores[head] = dot_nt(qc[q_rows, cols], kbuf[keys, cols])
+        totals = []
+        for head in heads:
+            parts = [scores[head, :, i * HALF : (i + 1) * HALF] for i in range(5)]
             parts[0] = jnp.where(keep_old, parts[0], MASKED)
             parts[4] = jnp.where(keep_own, parts[4], MASKED)
             if edge_block:
                 for i in range(4):
                     absent = (sequence == 0) & (base + i * HALF < WINDOW)
                     parts[i] = jnp.where(absent, MASKED, parts[i])
-            masked = jnp.concatenate(parts, axis=1)
-            top = jnp.max(masked, axis=1, keepdims=True)
-            weights = jnp.exp2((masked - top) * EXP2_SCALE)
-            total = jnp.sum(weights, axis=1, keepdims=True)
-            mixed = dot(weights.astype(BF16), vbuf[keys, cols])
-            attn = (mixed / total).astype(BF16)
+            top = jnp.max(functools.reduce(jnp.maximum, parts), axis=1, keepdims=True)
+            total = None
+            for i in range(5):
+                weight = jnp.exp2((parts[i] - top) * EXP2_SCALE)
+                rounded[head, :, i * HALF : (i + 1) * HALF] = weight.astype(BF16)
+                total = weight if total is None else total + weight
+            totals.append(jnp.sum(total, axis=1, keepdims=True))
+        for head in heads:
+            cols = pl.ds(head * AHD, AHD)
+            mixed = dot(rounded[head], vbuf[keys, cols])
+            attn = (mixed / totals[head]).astype(BF16)
             out[o_rows, cols] = (attn.astype(F32) + fast[q_rows, cols].astype(F32)).astype(BF16)
 
     def edge_body(block, carry):
@@ -532,8 +516,8 @@
         attend(block, False)
         return carry
 
-    lax.fori_loop(0, 2, edge_body, 0)
-    lax.fori_loop(2, SPLIT, main_body, 0)
+    lax.fori_loop(0, 2, edge_body, 0, unroll=2)
+    lax.fori_loop(2, SPLIT, main_body, 0, unroll=2)
     copy = pltpu.make_async_copy(out, out_hbm, out_sem)
     copy.start()
     copy.wait()
@@ -558,7 +542,7 @@
             pltpu.VMEM((HID, FDIM), BF16),
             pltpu.VMEM((FDIM, HID), BF16),
             pltpu.VMEM((FDIM, HID), BF16),
-            pltpu.VMEM((HID, FDIM), BF16),
+            pltpu.VMEM((FDIM, HID), BF16),
             pltpu.VMEM((SPLIT, FDIM), F32),
             pltpu.VMEM((5 * HALF, HID), BF16),
             pltpu.VMEM((rows, FDIM), F32),
@@ -566,6 +550,8 @@
             pltpu.VMEM((rows, FDIM), BF16),
             pltpu.SemaphoreType.DMA((33,)),
             pltpu.SemaphoreType.DMA,
+            pltpu.VMEM((FDIM // AHD, HALF, WINDOW + HALF), F32),
+            pltpu.VMEM((FDIM // AHD, HALF, WINDOW + HALF), BF16),
         ],
         compiler_params=pltpu.CompilerParams(vmem_limit_bytes=VMEM_LIMIT),
         cost_estimate=pl.CostEstimate(
@@ -584,26 +570,28 @@
     ]
     tok_count = lax.axis_size("tok")
 
-    def across_core(array):
-        return lax.ppermute(array, "tok", [(i, i ^ 1) for i in range(tok_count)])
-
     def along(array, slot):
         return lax.ppermute(array, "head", [(i, (i + slot) % CHIPS) for i in range(CHIPS)])
 
+    def across(array, slot):
+        pairs = [
+            (t * CHIPS + i, (t ^ 1) * CHIPS + (i + slot) % CHIPS)
+            for t in range(tok_count)
+            for i in range(CHIPS)
+        ]
+        return lax.ppermute(array, AXES, pairs)
+
     def next_segment(array):
         return lax.ppermute(array, "tok", [(i, i + 2) for i in range(tok_count - 2)])
 
     order = (1, 3, 2)
-    own_kv, swap_kv = pack_kv(keys, values, token_rates.T)
-    other_kv = across_core(swap_kv)
-    owns, others = [own_kv[0]] * CHIPS, [other_kv[0]] * CHIPS
+    own_kv, swap_kv, own_q, swap_q = pack(keys, values, queries, token_rates.T)
+    owns, others = [own_kv[0]] * CHIPS, [None] * CHIPS
     for slot in order:
         owns[slot] = along(own_kv[slot], slot)
-    queries, owns[0] = lax.optimization_barrier((queries, owns[0]))
-    own_q, swap_q = pack_q(queries)
-    other_q = across_core(swap_q)
-    for slot in order:
-        others[slot] = along(other_kv[slot], slot)
+    for slot in order + (0,):
+        others[slot] = across(swap_kv[slot], slot)
+    other_q = across(swap_q, 0)
     q_parts = [None] * CHIPS
     for slot in order:
         part = jnp.concatenate([own_q[slot], other_q[slot]], axis=0)

time: 168 us -> 151 us (0.90)
  Pallas kernels: 76.5 us -> 63.5 us
  starting transfers between devices: 35.9 us -> 29.4 us
  waiting for transfers between devices: 44.6 us -> 48.9 us
    ppermute x2 -> x5, waiting for transfers between devices: 0.98 us -> 19 us  [across(): return lax.ppermute(array, AXES, pairs)]
    ppermute x9 -> x6, waiting for transfers between devices: 28.7 us -> 13.8 us  [along(): lax.ppermute(array, 'head', [(i, (i + slot) % CHIPS) for i in range(CHIPS)])]
    ppermute x9 -> x6, starting transfers between devices: 20.2 us -> 8.13 us  [along(): lax.ppermute(array, 'head', [(i, (i + slot) % CHIPS) for i in range(CHIPS)])]
    pallas_call x2, Pallas kernels: 38.8 us -> 28 us  [apply_chunk(): pl.pallas_call(functools.partial(apply_kernel, chunk), name='apply_attend...]
    ppermute x2 -> x5, starting transfers between devices: 1.6 us -> 6.73 us  [across(): return lax.ppermute(array, AXES, pairs)]
    pallas_call x2 -> x1, Pallas kernels: 7.56 us -> 5.84 us  [pack(): pl.pallas_call(pack_kernel, name='pack', out_shape=(kv_shape,) * (2 * CHI...]
  transfers between devices with their start and end apart: 14 -> 14, of which waited for: 5 -> 7; matrix products, arithmetic and copies ran while one was open for 5% -> 4% of each run, Pallas kernels for 31% -> 29%
where the time goes in v2:
time: 151 us
  Pallas kernels  63.5 us (42%)
  waiting for transfers between devices  48.9 us (32%)
  starting transfers between devices  29.4 us (19%)
  other arithmetic  5.74 us (4%)
  local copies, waits for them, and re-layouts  3.11 us (2%)
    pallas_call x1, Pallas kernels, fast_update(): pl.pallas_call(update_kernel, name='fast_update', out_shape=(jax.ShapeDty...  29.7 us
    pallas_call x2, Pallas kernels, apply_chunk(): pl.pallas_call(functools.partial(apply_kernel, chunk), name='apply_attend...  28 us
    ppermute x5, waiting for transfers between devices, across(): return lax.ppermute(array, AXES, pairs)  19 us
    all_to_all x2, waiting for transfers between devices, body(): lax.all_to_all(out, AXES, split_axis=0, concat_axis=1, tiled=True, axis_i...  16.1 us
    ppermute x6, waiting for transfers between devices, along(): lax.ppermute(array, 'head', [(i, (i + slot) % CHIPS) for i in range(CHIPS)])  13.8 us
    all_to_all x2, starting transfers between devices, body(): lax.all_to_all(out, AXES, split_axis=0, concat_axis=1, tiled=True, axis_i...  10.8 us
    ppermute x6, starting transfers between devices, along(): lax.ppermute(array, 'head', [(i, (i + slot) % CHIPS) for i in range(CHIPS)])  8.13 us
    ppermute x5, starting transfers between devices, across(): return lax.ppermute(array, AXES, pairs)  6.73 us
  transfers between devices with their start and end apart: 14, of which 7 were waited for; matrix products, arithmetic and copies ran while one was open for 4% of the time, Pallas kernels for 29%

profile of v2, /device:TPU:1, one launch (start us, length us, event | category | flops | bytes accessed | tf_op | source)
XLA Modules:
  0.0 150.9 jit_solution(14388841095533652811)
XLA Ops:
  0.0 5.8 %pack.1 = (bf16[528,512]{1,0:T(8,128)(2,1)}, bf16[528,512]{1,0:T(8,128)(2,1)}, bf16[528,512]{1,0:T(8,128)(2,1)}, bf16[528,512]{1,0:T(8,128)(2,1)}, bf16[528,512]...) custom-call(bf16[256,4096]{1,0:T(8,128)(2,1)} %keys.1, ...), custom_call_target="tpu_custom_call" | custom-call | bytes 24000000 | tf_op jit(solution)/shard_map/pack/pallas_call | solution.py:118
  5.8 1.5 collective-permute-start
  7.3 2.8 %collective-permute-start.3 = (bf16[528,512]{1,0:T(8,128)(2,1)}, bf16[528,512]{1,0:T(8,128)(2,1)S(1)}, u32[]{:S(2)}, u32[]{:S(2)}) collective-permute-start(bf16[528,512]{1,0:T(8,128)(2,1)} %get-tuple-element.28), channel_id=1, source_target_pairs={{0,6},{1,7},{2,4},{3,5},{4,2},{5,3},{6,0},{7,1},{8,14},{9,15},{10,... | collective-permute-start | bytes 1622024 | tf_op jit(solution)/shard_map/ppermute | solution.py:582
  10.2 1.2 collective-permute-start.5
  11.3 0.6 collective-permute-start.1
  11.9 0.3 collective-permute-start.7
  12.2 0.0 copy-done.7
  12.2 0.6 reshape.9.gain_hbm
  12.8 1.2 slice_bitcast_fusion.3
  14.0 9.7 %collective-permute-done.3.other2 = bf16[528,512]{1,0:T(8,128)(2,1)S(1)} collective-permute-done((bf16[528,512]{1,0:T(8,128)(2,1)}, bf16[528,512]{1,0:T(8,128)(2,1)S(1)}, u32[]{:S(2)}, u32[]{:S(2)}) %collective-permute-start.3) | collective-permute-done | bytes 540704 | tf_op jit(solution)/shard_map/ppermute | solution.py:582
  23.6 2.8 %collective-permute-start.8 = (bf16[528,512]{1,0:T(8,128)(2,1)}, bf16[528,512]{1,0:T(8,128)(2,1)S(1)}, u32[]{:S(2)}, u32[]{:S(2)}) collective-permute-start(bf16[528,512]{1,0:T(8,128)(2,1)} %get-tuple-element.34), channel_id=1, source_target_pairs={{0,2},{1,3},{2,0},{3,1},{4,6},{5,7},{6,4},{7,5},{8,10},{9,11},{10,... | collective-permute-start | bytes 1622024 | tf_op jit(solution)/shard_map/ppermute | solution.py:574
  26.5 9.3 %collective-permute-done.5.other3 = bf16[528,512]{1,0:T(8,128)(2,1)S(1)} collective-permute-done((bf16[528,512]{1,0:T(8,128)(2,1)}, bf16[528,512]{1,0:T(8,128)(2,1)S(1)}, u32[]{:S(2)}, u32[]{:S(2)}) %collective-permute-start.5) | collective-permute-done | bytes 540704 | tf_op jit(solution)/shard_map/ppermute | solution.py:582
  35.8 2.2 %collective-permute-start.9 = (bf16[528,512]{1,0:T(8,128)(2,1)}, bf16[528,512]{1,0:T(8,128)(2,1)S(1)}, u32[]{:S(2)}, u32[]{:S(2)}) collective-permute-start(bf16[528,512]{1,0:T(8,128)(2,1)} %get-tuple-element.35), channel_id=1, source_target_pairs={{0,3},{1,0},{2,1},{3,2},{4,7},{5,4},{6,5},{7,6},{8,11},{9,8},{10,9... | collective-permute-start | bytes 1622024 | tf_op jit(solution)/shard_map/ppermute | solution.py:574
  38.0 0.0 collective-permute-done.other_q
  38.0 0.7 collective-permute-start.10
  38.6 0.1 slice_bitcast_fusion
  38.7 0.9 pad_maximum_fusion.4
  39.5 0.9 pad_maximum_fusion.3
  40.4 0.8 pad_maximum_fusion.2
  41.2 0.0 collective-permute-done.1.other1
  41.2 0.0 collective-permute-start.2
  41.2 5.8 %collective-permute-done.7.own1 = bf16[528,512]{1,0:T(8,128)(2,1)} collective-permute-done((bf16[528,512]{1,0:T(8,128)(2,1)}, bf16[528,512]{1,0:T(8,128)(2,1)}, u32[]{:S(2)}, u32[]{:S(2)}) %collective-permute-start.7) | collective-permute-done | bytes 540704 | tf_op jit(solution)/shard_map/ppermute | solution.py:574
  47.0 2.8 %collective-permute-start.4 = (bf16[512,512]{1,0:T(8,128)(2,1)}, bf16[512,512]{1,0:T(8,128)(2,1)}, u32[]{:S(2)}, u32[]{:S(2)}) collective-permute-start(bf16[512,512]{1,0:T(8,128)(2,1)} %pad_maximum_fusion.3), channel_id=1, source_target_pairs={{0,2},{1,3},{2,0},{3,1},{4,6},{5,7},{6,4},{7,5},{8,10},{9,11},{10,... | collective-permute-start | bytes 1572872 | tf_op jit(solution)/shard_map/ppermute | solution.py:574
  49.8 7.8 %collective-permute-done.8.own2 = bf16[528,512]{1,0:T(8,128)(2,1)S(1)} collective-permute-done((bf16[528,512]{1,0:T(8,128)(2,1)}, bf16[528,512]{1,0:T(8,128)(2,1)S(1)}, u32[]{:S(2)}, u32[]{:S(2)}) %collective-permute-start.8) | collective-permute-done | bytes 540704 | tf_op jit(solution)/shard_map/ppermute | solution.py:574
  57.6 0.0 collective-permute-start.6
  57.6 0.3 collective-permute-done.9.own3
  57.9 0.0 collective-permute-done.10.other0
  57.9 0.0 copy-done.3
  57.9 0.0 copy-done.1
  57.9 1.6 %select_select_fusion.1 = (bf16[528,512]{1,0:T(8,128)(2,1)S(1)}, bf16[528,512]{1,0:T(8,128)(2,1)S(1)}) fusion(pred[]{:T(512)S(6)} %eq.22, pred[]{:T(512)S(6)} %eq.21, pred[]{:T(512)S(6)} %eq.19, bf16[528,512]{1,0:T(8,128)(2,1)S(1)} %collective-permute-done.3.other2, bf16[528,512]{1,0:T(8,128)(2,1)S(1)} %collective-permute-done.8.own2, pred[]{:T(512)S(6)} %eq.20, ...), kind=kLoop, calls=%fused_computation.3 | loop fusion | flops 2703360 | bytes 5406725 | tf_op jit(solution)/shard_map/jit(_where)/select_n | solution.py:607
  59.6 0.1 fusion
  59.7 0.1 pad_maximum_fusion.1
  59.8 3.8 %collective-permute-start.11 = (bf16[1024,512]{1,0:T(8,128)(2,1)S(1)}, bf16[1024,512]{1,0:T(8,128)(2,1)S(1)}, u32[]{:S(2)}, u32[]{:S(2)}) collective-permute-start(bf16[1024,512]{1,0:T(8,128)(2,1)S(1)} %pad_maximum_fusion.1), channel_id=1, source_target_pairs={{0,8},{4,12},{8,16},{12,20},{16,24},{20,28},{24,32},{28,36},{32,40... | collective-permute-start | bytes 3145736 | tf_op jit(solution)/shard_map/ppermute | solution.py:585
  63.6 29.7 %fast_update.1 = (bf16[512,1024]{1,0:T(8,128)(2,1)}, bf16[512,1024]{1,0:T(8,128)(2,1)}, bf16[512,1024]{1,0:T(8,128)(2,1)}) custom-call(s32[16]{0:T(128)} %bounds.5, bf16[528,512]{1,0:T(8,128)(2,1)} %get-tuple-element.32.own0, bf16[528,512]{1,0:T(8,128)(2,1)} %collective-permute-done.7.own1, bf16[528,512]{1,0:T(8,128)(2,1)} %copy-done.4, ...), custom_call_target="tpu_custom_call" | custom-call | flops 20000000000 | bytes 12000000 | tf_op jit(solution)/shard_map/fast_update/pallas_call | solution.py:308
  93.2 0.0 collective-permute-done.2.q1
  93.2 0.0 collective-permute-done.4.q2
  93.2 0.0 collective-permute-done.6.q3
  93.3 0.0 collective-permute-done.11.halo
  93.3 1.0 copy-done.8
  94.3 14.0 %apply_attend.3 = bf16[1024,512]{1,0:T(8,128)(2,1)} custom-call(s32[16]{0:T(128)} %bounds.5, bf16[4,256,512]{2,1,0:T(8,128)(2,1)} %get-tuple-element.24.own_q, bf16[4,256,512]{2,1,0:T(8,128)(2,1)} %copy-done, bf16[512,512]{1,0:T(8,128)(2,1)} %collective-permute-done.2.q1, bf16[512,512]{1,0:T(8,128)(2,1)} %collective-permute-done.4.q2, ...), custom_call_target="tpu_custom_call" | custom-call | flops 8000000000 | bytes 14000000 | tf_op jit(solution)/shard_map/apply_attend/pallas_call | solution.py:529
  108.3 6.5 %all-to-all-start.1 = ((bf16[8,128,512]{2,1,0:T(8,128)(2,1)}), bf16[8,128,512]{2,1,0:T(8,128)(2,1)S(1)}, u32[]{:S(2)}, u32[]{:S(2)}) async-start(bf16[8,128,512]{2,1,0:T(8,128)(2,1)} %bitcast.26), calls=%async_computation.1 | async-start | bytes 2097152 | tf_op jit(solution)/shard_map/all_to_all | solution.py:635
  114.7 14.0 %apply_attend.2 = bf16[1024,512]{1,0:T(8,128)(2,1)} custom-call(s32[16]{0:T(128)} %bounds.5, bf16[4,256,512]{2,1,0:T(8,128)(2,1)} %get-tuple-element.24.own_q, bf16[4,256,512]{2,1,0:T(8,128)(2,1)} %copy-done, bf16[512,512]{1,0:T(8,128)(2,1)} %collective-permute-done.2.q1, bf16[512,512]{1,0:T(8,128)(2,1)} %collective-permute-done.4.q2, ...), custom_call_target="tpu_custom_call" | custom-call | flops 8000000000 | bytes 14000000 | tf_op jit(solution)/shard_map/apply_attend/pallas_call | solution.py:529
  128.7 1.1 all-to-all-done.1
  129.8 4.3 %all-to-all-start = ((bf16[8,128,512]{2,1,0:T(8,128)(2,1)}), bf16[8,128,512]{2,1,0:T(8,128)(2,1)S(1)}, u32[]{:S(2)}, u32[]{:S(2)}) async-start(bf16[8,128,512]{2,1,0:T(8,128)(2,1)} %bitcast.25), calls=%async_computation | async-start | bytes 2097152 | tf_op jit(solution)/shard_map/all_to_all | solution.py:635
  134.2 0.1 copy.13
  134.3 15.0 %all-to-all-done = bf16[8,128,512]{2,1,0:T(8,128)(2,1)S(1)} async-done(((bf16[8,128,512]{2,1,0:T(8,128)(2,1)}), bf16[8,128,512]{2,1,0:T(8,128)(2,1)S(1)}, u32[]{:S(2)}, u32[]{:S(2)}) %all-to-all-start) | async-done | bytes 1048608 | tf_op jit(solution)/shard_map/all_to_all | solution.py:635
  149.3 0.1 copy.12
  149.4 1.5 pad_maximum_fusion
  (14 shorter events, 0.0 us)
Async XLA Ops:
  0.0 12.2 %copy-start.7 = (f32[4096]{0:T(1024)S(1)}, f32[4096]{0:T(1024)}, u32[]{:S(2)}) copy-start(f32[4096]{0:T(1024)} %param.16) | copy-start | bytes 49156
  5.8 32.1 %collective-permute-start = (bf16[4,256,512]{2,1,0:T(8,128)(2,1)}, bf16[4,256,512]{2,1,0:T(8,128)(2,1)S(1)}, u32[]{:S(2)}, u32[]{:S(2)}) collective-permute-start(bf16[4,256,512]{2,1,0:T(8,128)(2,1)} %get-tuple-element.25), channel_id=1, source_target_pairs={{0,4},{1,5},{2,6},{3,7},{4,0},{5,1},{6,2},{7,3},{8,12},{9,13},{10,... | collective-permute-start | bytes 3145736 | tf_op jit(solution)/shard_map/ppermute | solution.py:582
  7.3 16.3 %collective-permute-start.3 = (bf16[528,512]{1,0:T(8,128)(2,1)}, bf16[528,512]{1,0:T(8,128)(2,1)S(1)}, u32[]{:S(2)}, u32[]{:S(2)}) collective-permute-start(bf16[528,512]{1,0:T(8,128)(2,1)} %get-tuple-element.28), channel_id=1, source_target_pairs={{0,6},{1,7},{2,4},{3,5},{4,2},{5,3},{6,0},{7,1},{8,14},{9,15},{10,... | collective-permute-start | bytes 1622024 | tf_op jit(solution)/shard_map/ppermute | solution.py:582
  10.2 25.6 %collective-permute-start.5 = (bf16[528,512]{1,0:T(8,128)(2,1)}, bf16[528,512]{1,0:T(8,128)(2,1)S(1)}, u32[]{:S(2)}, u32[]{:S(2)}) collective-permute-start(bf16[528,512]{1,0:T(8,128)(2,1)} %get-tuple-element.30), channel_id=1, source_target_pairs={{0,7},{1,4},{2,5},{3,6},{4,3},{5,0},{6,1},{7,2},{8,15},{9,12},{10,... | collective-permute-start | bytes 1622024 | tf_op jit(solution)/shard_map/ppermute | solution.py:582
  11.3 29.9 %collective-permute-start.1 = (bf16[528,512]{1,0:T(8,128)(2,1)}, bf16[528,512]{1,0:T(8,128)(2,1)}, u32[]{:S(2)}, u32[]{:S(2)}) collective-permute-start(bf16[528,512]{1,0:T(8,128)(2,1)} %get-tuple-element.26), channel_id=1, source_target_pairs={{0,5},{1,6},{2,7},{3,4},{4,1},{5,2},{6,3},{7,0},{8,13},{9,14},{10,... | collective-permute-start | bytes 1622024 | tf_op jit(solution)/shard_map/ppermute | solution.py:582
  11.9 35.1 %collective-permute-start.7 = (bf16[528,512]{1,0:T(8,128)(2,1)}, bf16[528,512]{1,0:T(8,128)(2,1)}, u32[]{:S(2)}, u32[]{:S(2)}) collective-permute-start(bf16[528,512]{1,0:T(8,128)(2,1)} %get-tuple-element.33), channel_id=1, source_target_pairs={{0,1},{1,2},{2,3},{3,0},{4,5},{5,6},{6,7},{7,4},{8,9},{9,10},{10,1... | collective-permute-start | bytes 1622024 | tf_op jit(solution)/shard_map/ppermute | solution.py:574
  23.6 34.3 %copy-start.2 = (bf16[528,512]{1,0:T(8,128)(2,1)}, bf16[528,512]{1,0:T(8,128)(2,1)S(1)}, u32[]{:S(2)}) copy-start(bf16[528,512]{1,0:T(8,128)(2,1)S(1)} %collective-permute-done.3.other2) | copy-start | bytes 1622020
  23.6 34.0 %collective-permute-start.8 = (bf16[528,512]{1,0:T(8,128)(2,1)}, bf16[528,512]{1,0:T(8,128)(2,1)S(1)}, u32[]{:S(2)}, u32[]{:S(2)}) collective-permute-start(bf16[528,512]{1,0:T(8,128)(2,1)} %get-tuple-element.34), channel_id=1, source_target_pairs={{0,2},{1,3},{2,0},{3,1},{4,6},{5,7},{6,4},{7,5},{8,10},{9,11},{10,... | collective-permute-start | bytes 1622024 | tf_op jit(solution)/shard_map/ppermute | solution.py:574
  35.8 22.1 %copy-start.3 = (bf16[528,512]{1,0:T(8,128)(2,1)}, bf16[528,512]{1,0:T(8,128)(2,1)S(1)}, u32[]{:S(2)}) copy-start(bf16[528,512]{1,0:T(8,128)(2,1)S(1)} %collective-permute-done.5.other3) | copy-start | bytes 1622020
  35.8 22.1 %collective-permute-start.9 = (bf16[528,512]{1,0:T(8,128)(2,1)}, bf16[528,512]{1,0:T(8,128)(2,1)S(1)}, u32[]{:S(2)}, u32[]{:S(2)}) collective-permute-start(bf16[528,512]{1,0:T(8,128)(2,1)} %get-tuple-element.35), channel_id=1, source_target_pairs={{0,3},{1,0},{2,1},{3,2},{4,7},{5,4},{6,5},{7,6},{8,11},{9,8},{10,9... | collective-permute-start | bytes 1622024 | tf_op jit(solution)/shard_map/ppermute | solution.py:574
  38.0 3.3 %copy-start = (bf16[4,256,512]{2,1,0:T(8,128)(2,1)}, bf16[4,256,512]{2,1,0:T(8,128)(2,1)S(1)}, u32[]{:S(2)}) copy-start(bf16[4,256,512]{2,1,0:T(8,128)(2,1)S(1)} %collective-permute-done.other_q) | copy-start | bytes 3145732
  38.0 20.0 %copy-start.1 = (bf16[528,512]{1,0:T(8,128)(2,1)S(1)}, bf16[528,512]{1,0:T(8,128)(2,1)}, u32[]{:S(2)}) copy-start(bf16[528,512]{1,0:T(8,128)(2,1)} %get-tuple-element.32.own0) | copy-start | bytes 1622020
  38.0 19.9 %collective-permute-start.10 = (bf16[528,512]{1,0:T(8,128)(2,1)}, bf16[528,512]{1,0:T(8,128)(2,1)S(1)}, u32[]{:S(2)}, u32[]{:S(2)}) collective-permute-start(bf16[528,512]{1,0:T(8,128)(2,1)} %get-tuple-element.36), channel_id=1, source_target_pairs={{0,4},{1,5},{2,6},{3,7},{4,0},{5,1},{6,2},{7,3},{8,12},{9,13},{10,... | collective-permute-start | bytes 1622024 | tf_op jit(solution)/shard_map/ppermute | solution.py:582
  41.2 52.0 %collective-permute-start.2 = (bf16[512,512]{1,0:T(8,128)(2,1)}, bf16[512,512]{1,0:T(8,128)(2,1)}, u32[]{:S(2)}, u32[]{:S(2)}) collective-permute-start(bf16[512,512]{1,0:T(8,128)(2,1)} %pad_maximum_fusion.2), channel_id=1, source_target_pairs={{0,1},{1,2},{2,3},{3,0},{4,5},{5,6},{6,7},{7,4},{8,9},{9,10},{10,1... | collective-permute-start | bytes 1572872 | tf_op jit(solution)/shard_map/ppermute | solution.py:574
  47.0 46.2 %collective-permute-start.4 = (bf16[512,512]{1,0:T(8,128)(2,1)}, bf16[512,512]{1,0:T(8,128)(2,1)}, u32[]{:S(2)}, u32[]{:S(2)}) collective-permute-start(bf16[512,512]{1,0:T(8,128)(2,1)} %pad_maximum_fusion.3), channel_id=1, source_target_pairs={{0,2},{1,3},{2,0},{3,1},{4,6},{5,7},{6,4},{7,5},{8,10},{9,11},{10,... | collective-permute-start | bytes 1572872 | tf_op jit(solution)/shard_map/ppermute | solution.py:574
  57.6 2.0 %copy-start.4 = (bf16[528,512]{1,0:T(8,128)(2,1)}, bf16[528,512]{1,0:T(8,128)(2,1)S(1)}, u32[]{:S(2)}) copy-start(bf16[528,512]{1,0:T(8,128)(2,1)S(1)} %collective-permute-done.8.own2) | copy-start | bytes 1622020
  57.6 35.6 %collective-permute-start.6 = (bf16[512,512]{1,0:T(8,128)(2,1)}, bf16[512,512]{1,0:T(8,128)(2,1)}, u32[]{:S(2)}, u32[]{:S(2)}) collective-permute-start(bf16[512,512]{1,0:T(8,128)(2,1)} %pad_maximum_fusion.4), channel_id=1, source_target_pairs={{0,3},{1,0},{2,1},{3,2},{4,7},{5,4},{6,5},{7,6},{8,11},{9,8},{10,9... | collective-permute-start | bytes 1572872 | tf_op jit(solution)/shard_map/ppermute | solution.py:574
  57.9 1.7 %copy-start.5 = (bf16[528,512]{1,0:T(8,128)(2,1)}, bf16[528,512]{1,0:T(8,128)(2,1)S(1)}, u32[]{:S(2)}) copy-start(bf16[528,512]{1,0:T(8,128)(2,1)S(1)} %collective-permute-done.9.own3) | copy-start | bytes 1622020
  57.9 1.7 %copy-start.6 = (bf16[528,512]{1,0:T(8,128)(2,1)}, bf16[528,512]{1,0:T(8,128)(2,1)S(1)}, u32[]{:S(2)}) copy-start(bf16[528,512]{1,0:T(8,128)(2,1)S(1)} %collective-permute-done.10.other0) | copy-start | bytes 1622020
  59.8 33.5 %collective-permute-start.11 = (bf16[1024,512]{1,0:T(8,128)(2,1)S(1)}, bf16[1024,512]{1,0:T(8,128)(2,1)S(1)}, u32[]{:S(2)}, u32[]{:S(2)}) collective-permute-start(bf16[1024,512]{1,0:T(8,128)(2,1)S(1)} %pad_maximum_fusion.1), channel_id=1, source_target_pairs={{0,8},{4,12},{8,16},{12,20},{16,24},{20,28},{24,32},{28,36},{32,40... | collective-permute-start | bytes 3145736 | tf_op jit(solution)/shard_map/ppermute | solution.py:585
  93.3 1.0 copy-start.8
  108.3 21.6 %all-to-all-start.1 = ((bf16[8,128,512]{2,1,0:T(8,128)(2,1)}), bf16[8,128,512]{2,1,0:T(8,128)(2,1)S(1)}, u32[]{:S(2)}, u32[]{:S(2)}) async-start(bf16[8,128,512]{2,1,0:T(8,128)(2,1)} %bitcast.26), calls=%async_computation.1 | async-start | bytes 2097152 | tf_op jit(solution)/shard_map/all_to_all | solution.py:635
  129.8 19.4 %all-to-all-start = ((bf16[8,128,512]{2,1,0:T(8,128)(2,1)}), bf16[8,128,512]{2,1,0:T(8,128)(2,1)S(1)}, u32[]{:S(2)}, u32[]{:S(2)}) async-start(bf16[8,128,512]{2,1,0:T(8,128)(2,1)} %bitcast.25), calls=%async_computation | async-start | bytes 2097152 | tf_op jit(solution)/shard_map/all_to_all | solution.py:635
